TPU v7x, 32 devices: a whole 2x2x4 slice. The times are simulated.
32 devices in a mesh: groups: 1, wa: 32 (over z, y, x, core).
Axes of the slice: x: 2, y: 2, z: 4, core: 2. Of those that a mesh axis runs over, the one named last changes fastest.
Arguments:
- queries: bfloat16 [32, 1, 384, 1536], P(('groups', 'wa')), may hold values from -10 to 10
- keys_values: bfloat16 [2, 32, 1, 384, 1536], P(None, ('groups', 'wa')), may hold values from -10 to 10
- tile_visible: int32 [32, 1], P('groups'), may hold values 0 or 1
- out_weight: bfloat16 [1536, 3072], P(None, 'wa'), may hold values from -0.15625 to 0.15625
Outputs:
- mixed: bfloat16 [32, 1, 384, 3072], P(('groups', 'wa'))
All inputs are finite; a program needn't handle non-finite values.
Results may differ from a plain program's by a relative error of at most 0.0057.
Values may be sent and summed in bfloat16 or wider, within the bound.
No kernel may reach another device: no remote copies, remote signals or barrier semaphores. Data moves between devices by JAX's collectives and lax.ppermute only.
A program may use at most 128 MiB of HBM per device.

v0:
```python
import functools
import math

import jax
import jax.numpy as jnp
from jax import lax
from jax.experimental import pallas as pl
from jax.experimental.pallas import tpu as pltpu
from jax.sharding import PartitionSpec as P


HEAD_DIM = 128
GW = 8
CHUNKS = 4
STAT_ROWS = 16
BIG = 1e30


def pair_swaps(count, stride, parity, block):
    pairs = []
    for device in range(count):
        position = (device // stride) % block
        if position % 2 == parity % 2 and position + 1 < block:
            pairs.append((device, device + stride))
            pairs.append((device + stride, device))
    return pairs


def split_three(value):
    high = value.astype(jnp.bfloat16)
    rest = value - high.astype(jnp.float32)
    middle = rest.astype(jnp.bfloat16)
    low = (rest - middle.astype(jnp.float32)).astype(jnp.bfloat16)
    return high, middle, low


def attend_kernel(flags, q_own, q_even, q_odd, kv_own, kv_even, kv_odd, out_own, out_even, out_odd):
    tile = q_own.shape[0]
    block = 128
    rows = tile // block
    factor = HEAD_DIM ** (-0.5) * math.log2(math.e)
    keys = jnp.concatenate([kv_own[0], kv_even[0], kv_odd[0]], axis=0)
    values = jnp.concatenate([kv_own[1], kv_even[1], kv_odd[1]], axis=0)
    values = jnp.concatenate([values, jnp.ones_like(values)], axis=1)
    places = ((q_own, out_own), (q_even, out_even), (q_odd, out_odd))
    diagonal = lax.broadcasted_iota(jnp.int32, (block, block), 0) == lax.broadcasted_iota(
        jnp.int32, (block, block), 1
    )

    def score(place, i):
        query = places[place][0][i * block : (i + 1) * block, :]
        return lax.dot_general(query, keys, (((1,), (1,)), ((), ())), preferred_element_type=jnp.float32)

    def finish(place, i, scores):
        out_ref = places[place][1]
        seen = (flags[0] if place == 0 else flags[1], flags[2], flags[3])
        parts = [scores[:, t * tile : (t + 1) * tile] for t in range(3)]
        peaks = [
            jnp.where(seen[t] == 1, jnp.max(parts[t], axis=1, keepdims=True) * factor, -BIG) for t in range(3)
        ]
        peak = jnp.maximum(jnp.maximum(peaks[0], peaks[1]), peaks[2])
        weights = [jnp.exp2(parts[t] * factor - jnp.where(seen[t] == 1, peak, BIG)) for t in range(3)]
        low = jnp.concatenate([w.astype(jnp.bfloat16) for w in weights], axis=1)
        summed = jnp.dot(low, values, preferred_element_type=jnp.float32)
        total = summed[:, HEAD_DIM:]
        some = total > 0.0
        safe = jnp.where(some, total, 1.0)
        out_ref[i * block : (i + 1) * block, :] = (summed[:, :HEAD_DIM] / safe).astype(out_ref.dtype)
        level = jnp.where(some, peak + jnp.log2(safe), -BIG)
        return jnp.sum(jnp.where(diagonal, level, 0.0), axis=0, keepdims=True)

    def store(place, stats):
        out_ref = places[place][1]
        stat = jnp.concatenate(stats, axis=0)
        if out_ref.dtype == jnp.float32:
            packed = [stat, jnp.zeros((STAT_ROWS - rows, block), jnp.float32)]
        else:
            packed = [p.astype(jnp.float32) for p in split_three(stat)]
            packed.append(jnp.zeros((STAT_ROWS - 3 * rows, block), jnp.float32))
        out_ref[tile : tile + STAT_ROWS, :] = jnp.concatenate(packed, axis=0).astype(out_ref.dtype)

    order = [(place, i) for place in range(3) for i in range(rows)]
    stats = {}
    ahead = score(*order[0])
    for n, (place, i) in enumerate(order):
        scores = ahead
        if n + 1 < len(order):
            ahead = score(*order[n + 1])
        stats.setdefault(place, []).append(finish(place, i, scores))
        if i == rows - 1:
            store(place, stats[place])


def attend(flags, queries, kv_own, kv_near, first_head, heads):
    tile = kv_own.shape[1]
    q_spec = pl.BlockSpec((tile, HEAD_DIM), lambda h, f: (0, first_head + h))
    own_spec = pl.BlockSpec((2, tile, HEAD_DIM), lambda h, f: (0, 0, first_head + h))
    near_spec = pl.BlockSpec((2, tile, HEAD_DIM), lambda h, f: (0, 0, h))
    out_spec = pl.BlockSpec((tile + STAT_ROWS, HEAD_DIM), lambda h, f: (0, h))
    shape = (tile + STAT_ROWS, heads * HEAD_DIM)
    pair_count = 9 * tile * tile * heads
    return pl.pallas_call(
        attend_kernel,
        grid_spec=pltpu.PrefetchScalarGridSpec(
            num_scalar_prefetch=1,
            grid=(heads,),
            in_specs=[q_spec] * 3 + [own_spec] + [near_spec] * 2,
            out_specs=[out_spec] * 3,
        ),
        out_shape=[
            jax.ShapeDtypeStruct(shape, jnp.float32),
            jax.ShapeDtypeStruct(shape, jnp.bfloat16),
            jax.ShapeDtypeStruct(shape, jnp.bfloat16),
        ],
        cost_estimate=pl.CostEstimate(
            flops=pair_count * HEAD_DIM * 4,
            transcendentals=pair_count,
            bytes_accessed=heads * HEAD_DIM * tile * 2 * 13,
        ),
        name="attend",
    )(flags, *queries, kv_own, *kv_near)


def merge_kernel(edge, own, even, odd, attended):
    tile = attended.shape[0]
    block = 128
    rows = tile // block
    levels = [own[tile : tile + rows, :]]
    for ref in (even, odd):
        stat = ref[tile : tile + STAT_ROWS, :].astype(jnp.float32)
        levels.append(stat[:rows] + stat[rows : 2 * rows] + stat[2 * rows : 3 * rows])
    levels[2] = jnp.where(edge[0] == 1, -BIG, levels[2])
    top = jnp.maximum(jnp.maximum(levels[0], levels[1]), levels[2])
    shares = [jnp.exp2(level - top) for level in levels]
    scale = 1.0 / (shares[0] + shares[1] + shares[2])
    for i in range(rows):
        span = slice(i * block, (i + 1) * block)
        mixed = None
        for ref, share in zip((own, even, odd), shares):
            wide = jnp.broadcast_to((share * scale)[i : i + 1, :], (block, block)).T
            part = ref[span, :].astype(jnp.float32) * wide
            mixed = part if mixed is None else mixed + part
        attended[span, :] = mixed.astype(jnp.bfloat16)


def merge(edge, own, even, odd):
    tile = own.shape[0] - STAT_ROWS
    heads = own.shape[1] // HEAD_DIM
    spec = pl.BlockSpec((tile + STAT_ROWS, HEAD_DIM), lambda h, e: (0, h))
    return pl.pallas_call(
        merge_kernel,
        grid_spec=pltpu.PrefetchScalarGridSpec(
            num_scalar_prefetch=1,
            grid=(heads,),
            in_specs=[spec] * 3,
            out_specs=pl.BlockSpec((tile, HEAD_DIM), lambda h, e: (0, h)),
        ),
        out_shape=jax.ShapeDtypeStruct((tile, heads * HEAD_DIM), jnp.bfloat16),
        cost_estimate=pl.CostEstimate(
            flops=tile * heads * HEAD_DIM * 8, transcendentals=0, bytes_accessed=tile * heads * HEAD_DIM * 10
        ),
        name="merge",
    )(edge, own, even, odd)


def project_kernel(masks, shard, group, edge_bit, *refs):
    count = len(masks)
    pieces = refs[:count]
    att_refs = refs[count:-3]
    out_ref, held, sem = refs[-3:]
    step = pl.program_id(0)
    me = lax.axis_index("wa")
    row = me // GW
    flip = jnp.where((row == 0) | (row == 3), edge_bit, 0)

    def move(ref, place, owner):
        target = pl.ds(pl.multiple_of(owner * shard, shard), shard)
        return pltpu.make_async_copy(ref.at[pl.ds(place * shard, shard)], held.at[target], sem.at[owner])

    @pl.when(step == 0)
    def _():
        for ref, mask in zip(pieces, masks):
            first = jnp.bitwise_xor(me, mask)
            if mask & (2 * GW):
                first = jnp.bitwise_xor(first, flip)
            for place in range(2):
                move(ref, place, jnp.bitwise_xor(first, place * GW)).start()

    for i in range(group):
        move(pieces[0], 0, step * group + i).wait()
    columns = pl.ds(pl.multiple_of(step * (group * shard), 128), group * shard)
    depth = 0
    total = None
    for ref in att_refs:
        width = ref.shape[1]
        part = lax.dot_general(
            ref[...],
            held[columns, depth : depth + width],
            (((1,), (1,)), ((), ())),
            preferred_element_type=jnp.float32,
        )
        total = part if total is None else total + part
        depth += width
    out_ref[...] = total.astype(jnp.bfloat16)


def project(attended, pieces, masks, shard, count):
    tile = attended[0].shape[0]
    depth = pieces[0].shape[1]
    group = 128 // math.gcd(128, shard)
    return pl.pallas_call(
        functools.partial(project_kernel, masks, shard, group, GW),
        grid=(count // group,),
        in_specs=[pl.BlockSpec(memory_space=pl.ANY)] * len(pieces)
        + [pl.BlockSpec(a.shape, lambda g: (0, 0)) for a in attended],
        out_specs=pl.BlockSpec((tile, group * shard), lambda g: (0, g)),
        out_shape=jax.ShapeDtypeStruct((tile, count * shard), jnp.bfloat16),
        scratch_shapes=[pltpu.VMEM((count * shard, depth), jnp.bfloat16), pltpu.SemaphoreType.DMA((count,))],
        cost_estimate=pl.CostEstimate(
            flops=2 * tile * depth * count * shard, transcendentals=0, bytes_accessed=2 * depth * count * shard
        ),
        name="project",
    )(*pieces, *attended)


def passed(value, pairs):
    return lax.ppermute(value, "wa", pairs)


def gather_weight(own, count, row_even, row_odd, edge_row):
    def swap(value, bit):
        return passed(value, [(device, device ^ bit) for device in range(count)])

    ab = jnp.concatenate([own, passed(own, row_even)], axis=0)
    inner = passed(ab, row_odd)
    outer = passed(inner, [(d, d ^ GW) for d in range(count) if d // GW in (1, 2)])
    cd = jnp.where(edge_row, outer, inner)
    pieces = {"ab": ab, "cd": cd}
    masks = {"ab": 0, "cd": 3 * GW}
    for bit, mark in ((2, "x"), (4, "y"), (1, "c")):
        for name in list(pieces):
            pieces[mark + name] = swap(pieces[name], bit)
            masks[mark + name] = masks[name] ^ bit
    return list(pieces.values()), tuple(masks.values())


def use_pieces(count, shard):
    return count == 4 * GW and shard % 16 == 0 and count % (128 // math.gcd(128, shard)) == 0


def local(queries, keys_values, tile_visible, out_weight):
    count = lax.axis_size("wa")
    grid_rows = count // GW
    me = lax.axis_index("wa")
    row, col = me // GW, me % GW
    time_tiles, _, width = queries.shape[1:]
    shard = out_weight.shape[1]

    row_even, row_odd = (pair_swaps(count, GW, parity, grid_rows) for parity in (0, 1))
    col_even, col_odd = (pair_swaps(count, 1, parity, GW) for parity in (0, 1))

    def partner(position, parity, limit):
        near = jnp.where(position % 2 == parity, position + 1, position - 1)
        return jnp.clip(near, 0, limit - 1), (near >= 0) & (near < limit)

    near_even, inside_even = partner(row, 0, grid_rows)
    near_odd, inside_odd = partner(row, 1, grid_rows)

    spread = use_pieces(count, shard)
    if spread:
        pieces, masks = gather_weight(out_weight.T, count, row_even, row_odd, (row == 0) | (row == 3))
    else:
        whole = lax.all_gather(out_weight, "wa", axis=1, tiled=True)

    head_count = width // HEAD_DIM
    chunks = [head_count // CHUNKS + (j < head_count % CHUNKS) for j in range(CHUNKS)]
    outputs = []
    for t in range(time_tiles):
        marked = tile_visible[:, t]
        flags = jnp.stack(
            [
                jnp.int32(1),
                (marked[me] == 1).astype(jnp.int32),
                (inside_even & (marked[near_even * GW + col] == 1)).astype(jnp.int32),
                (inside_odd & (marked[near_odd * GW + col] == 1)).astype(jnp.int32),
            ]
        )
        query = queries[0, t]
        kv_own = keys_values[:, 0, t]
        near_queries = [passed(query, col_even), passed(query, col_odd)]
        first = 0
        partial = []
        for heads in chunks:
            cut = kv_own[:, :, first * HEAD_DIM : (first + heads) * HEAD_DIM]
            kv_near = [passed(cut, row_even), passed(cut, row_odd)]
            partial.append((first, heads, kv_near))
            first += heads
        attended = []
        edge = (col == 0) | (col == GW - 1)
        for first, heads, kv_near in partial:
            own, even, odd = attend(flags, [query] + near_queries, kv_own, kv_near, first, heads)
            even = passed(even, col_even)
            odd = passed(odd, col_odd)
            attended.append(merge(edge.astype(jnp.int32).reshape(1), own, even, odd))
        if spread:
            outputs.append(project(attended, pieces, masks, shard, count))
        else:
            outputs.append(
                jnp.dot(
                    jnp.concatenate(attended, axis=1), whole, preferred_element_type=jnp.float32
                ).astype(jnp.bfloat16)
            )
    return jnp.stack(outputs)[None]


def solution(mesh):
    in_specs = (
        P(("groups", "wa"), None, None, None),
        P(None, ("groups", "wa"), None, None, None),
        P("groups", None),
        P(None, "wa"),
    )
    out_specs = P(("groups", "wa"), None, None, None)

    return jax.shard_map(local, mesh=mesh, in_specs=in_specs, out_specs=out_specs, check_vma=False)
```

profile of v0, /device:TPU:13, one launch (start us, length us, event | category | flops | bytes accessed | tf_op | source)
XLA Modules:
  0.0 200.5 jit_solution(174251039404080033)
XLA Ops:
  3.5 3.3 %collective-permute-start.32 = (bf16[2,384,384]{2,1,0:T(8,128)(2,1)S(1)}, bf16[2,384,384]{2,1,0:T(8,128)(2,1)S(1)}, u32[]{:S(2)}, u32[]{:S(2)}) collective-permute-start(bf16[2,384,384]{2,1,0:T(8,128)(2,1)S(1)} %get-tuple-element.29), channel_id=1, source_target_pairs={{8,16},{16,8},{9,17},{17,9},{10,18},{18,10},{11,19},{19,11},{12,20... | collective-permute-start | bytes 1769480 | tf_op jit(solution)/shard_map/ppermute | solution.py:227
  9.1 11.6 %collective-permute-done.31.kv_even = bf16[2,384,384]{2,1,0:T(8,128)(2,1)S(1)} collective-permute-done((bf16[2,384,384]{2,1,0:T(8,128)(2,1)S(1)}, bf16[2,384,384]{2,1,0:T(8,128)(2,1)S(1)}, u32[]{:S(2)}, u32[]{:S(2)}) %collective-permute-start.31) | collective-permute-done | bytes 589856 | tf_op jit(solution)/shard_map/ppermute | solution.py:227
  20.7 3.2 %collective-permute-start.24 = (bf16[2,384,384]{2,1,0:T(8,128)(2,1)S(1)}, bf16[2,384,384]{2,1,0:T(8,128)(2,1)S(1)}, u32[]{:S(2)}, u32[]{:S(2)}) collective-permute-start(bf16[2,384,384]{2,1,0:T(8,128)(2,1)S(1)} %get-tuple-element.31), channel_id=1, source_target_pairs={{8,16},{16,8},{9,17},{17,9},{10,18},{18,10},{11,19},{19,11},{12,20... | collective-permute-start | bytes 1769480 | tf_op jit(solution)/shard_map/ppermute | solution.py:227
  24.1 9.3 %collective-permute-done.27.kv_even = bf16[2,384,384]{2,1,0:T(8,128)(2,1)S(1)} collective-permute-done((bf16[2,384,384]{2,1,0:T(8,128)(2,1)S(1)}, bf16[2,384,384]{2,1,0:T(8,128)(2,1)S(1)}, u32[]{:S(2)}, u32[]{:S(2)}) %collective-permute-start.27) | collective-permute-done | bytes 589856 | tf_op jit(solution)/shard_map/ppermute | solution.py:227
  33.4 3.2 %collective-permute-start.20 = (bf16[2,384,384]{2,1,0:T(8,128)(2,1)S(1)}, bf16[2,384,384]{2,1,0:T(8,128)(2,1)S(1)}, u32[]{:S(2)}, u32[]{:S(2)}) collective-permute-start(bf16[2,384,384]{2,1,0:T(8,128)(2,1)S(1)} %get-tuple-element.32), channel_id=1, source_target_pairs={{8,16},{16,8},{9,17},{17,9},{10,18},{18,10},{11,19},{19,11},{12,20... | collective-permute-start | bytes 1769480 | tf_op jit(solution)/shard_map/ppermute | solution.py:227
  39.6 6.4 %collective-permute-done.23.kv_even = bf16[2,384,384]{2,1,0:T(8,128)(2,1)S(1)} collective-permute-done((bf16[2,384,384]{2,1,0:T(8,128)(2,1)S(1)}, bf16[2,384,384]{2,1,0:T(8,128)(2,1)S(1)}, u32[]{:S(2)}, u32[]{:S(2)}) %collective-permute-start.23) | collective-permute-done | bytes 589856 | tf_op jit(solution)/shard_map/ppermute | solution.py:227
  49.2 5.9 %collective-permute-start.18 = (bf16[384,1536]{1,0:T(8,128)(2,1)S(1)}, bf16[384,1536]{1,0:T(8,128)(2,1)}, u32[]{:S(2)}, u32[]{:S(2)}) collective-permute-start(bf16[384,1536]{1,0:T(8,128)(2,1)S(1)} %bitcast.22), channel_id=1, source_target_pairs={{1,2},{2,1},{3,4},{4,3},{5,6},{6,5},{9,10},{10,9},{11,12},{12,11},... | collective-permute-start | bytes 3538952 | tf_op jit(solution)/shard_map/ppermute | solution.py:227
  55.2 3.6 %collective-permute-done.19.kv_even = bf16[2,384,384]{2,1,0:T(8,128)(2,1)S(1)} collective-permute-done((bf16[2,384,384]{2,1,0:T(8,128)(2,1)S(1)}, bf16[2,384,384]{2,1,0:T(8,128)(2,1)S(1)}, u32[]{:S(2)}, u32[]{:S(2)}) %collective-permute-start.19) | collective-permute-done | bytes 589856 | tf_op jit(solution)/shard_map/ppermute | solution.py:227
  60.2 9.4 %collective-permute-done.1 = bf16[192,1536]{1,0:T(8,128)(2,1)S(1)} collective-permute-done((bf16[192,1536]{1,0:T(8,128)(2,1)S(1)}, bf16[192,1536]{1,0:T(8,128)(2,1)S(1)}, u32[]{:S(2)}, u32[]{:S(2)}) %collective-permute-start.1) | collective-permute-done | bytes 589856 | tf_op jit(solution)/shard_map/ppermute | solution.py:227
  74.4 18.3 %collective-permute-done.3.refs_2_ = bf16[192,1536]{1,0:T(8,128)(2,1)} collective-permute-done((bf16[192,1536]{1,0:T(8,128)(2,1)S(1)}, bf16[192,1536]{1,0:T(8,128)(2,1)}, u32[]{:S(2)}, u32[]{:S(2)}) %collective-permute-start.3) | collective-permute-done | bytes 589856 | tf_op jit(solution)/shard_map/ppermute | solution.py:227
  95.7 9.6 %attend.7 = (f32[400,384]{1,0:T(8,128)}, bf16[400,384]{1,0:T(8,128)(2,1)}, bf16[400,384]{1,0:T(8,128)(2,1)}) custom-call(s32[4]{0:T(128)} %add_convert_fusion.flags, bf16[384,1536]{1,0:T(8,128)(2,1)} %bitcast.17, bf16[384,1536]{1,0:T(8,128)(2,1)} %collective-permute-done.17.q_even, bf16[384,1536]{1,0:T(8,128)(2,1)} %collective-permute-done.18.q_odd, ...), custom_call_target="tpu_custom_call" | custom-call | flops 2038431744 | bytes 3833856 | tf_op jit(solution)/shard_map/attend/pallas_call | solution.py:102
  108.2 4.4 %collective-permute-start.34 = (bf16[400,384]{1,0:T(8,128)(2,1)}, bf16[400,384]{1,0:T(8,128)(2,1)S(1)}, u32[]{:S(2)}, u32[]{:S(2)}) collective-permute-start(bf16[400,384]{1,0:T(8,128)(2,1)} %get-tuple-element.28), channel_id=1, source_target_pairs={{1,2},{2,1},{3,4},{4,3},{5,6},{6,5},{9,10},{10,9},{11,12},{12,11},... | collective-permute-start | bytes 921608 | tf_op jit(solution)/shard_map/ppermute | solution.py:227
  112.6 9.6 %attend.6 = (f32[400,384]{1,0:T(8,128)}, bf16[400,384]{1,0:T(8,128)(2,1)}, bf16[400,384]{1,0:T(8,128)(2,1)}) custom-call(s32[4]{0:T(128)} %add_convert_fusion.flags, bf16[384,1536]{1,0:T(8,128)(2,1)} %bitcast.18, bf16[384,1536]{1,0:T(8,128)(2,1)} %collective-permute-done.17.q_even, bf16[384,1536]{1,0:T(8,128)(2,1)} %collective-permute-done.18.q_odd, ...), custom_call_target="tpu_custom_call" | custom-call | flops 2038431744 | bytes 3833856 | tf_op jit(solution)/shard_map/attend/pallas_call | solution.py:102
  122.2 9.7 %attend.5 = (f32[400,384]{1,0:T(8,128)}, bf16[400,384]{1,0:T(8,128)(2,1)}, bf16[400,384]{1,0:T(8,128)(2,1)}) custom-call(s32[4]{0:T(128)} %add_convert_fusion.flags, bf16[384,1536]{1,0:T(8,128)(2,1)} %bitcast.19, bf16[384,1536]{1,0:T(8,128)(2,1)} %collective-permute-done.17.q_even, bf16[384,1536]{1,0:T(8,128)(2,1)} %collective-permute-done.18.q_odd, ...), custom_call_target="tpu_custom_call" | custom-call | flops 2038431744 | bytes 3833856 | tf_op jit(solution)/shard_map/attend/pallas_call | solution.py:102
  137.0 9.6 %attend.4 = (f32[400,384]{1,0:T(8,128)}, bf16[400,384]{1,0:T(8,128)(2,1)}, bf16[400,384]{1,0:T(8,128)(2,1)}) custom-call(s32[4]{0:T(128)} %add_convert_fusion.flags, bf16[384,1536]{1,0:T(8,128)(2,1)} %bitcast.20, bf16[384,1536]{1,0:T(8,128)(2,1)} %collective-permute-done.17.q_even, bf16[384,1536]{1,0:T(8,128)(2,1)} %collective-permute-done.18.q_odd, ...), custom_call_target="tpu_custom_call" | custom-call | flops 2038431744 | bytes 3833856 | tf_op jit(solution)/shard_map/attend/pallas_call | solution.py:102
  152.5 3.5 %collective-permute-done.26.odd = bf16[400,384]{1,0:T(8,128)(2,1)S(1)} collective-permute-done((bf16[400,384]{1,0:T(8,128)(2,1)}, bf16[400,384]{1,0:T(8,128)(2,1)S(1)}, u32[]{:S(2)}, u32[]{:S(2)}) %collective-permute-start.26) | collective-permute-done | bytes 307232 | tf_op jit(solution)/shard_map/ppermute | solution.py:227
  156.0 3.8 %collective-permute-start.10 = (bf16[192,1536]{1,0:T(8,128)(2,1)S(1)}, bf16[192,1536]{1,0:T(8,128)(2,1)}, u32[]{:S(2)}, u32[]{:S(2)}) collective-permute-start(bf16[192,1536]{1,0:T(8,128)(2,1)S(1)} %broadcast_select_fusion.refs_1_), channel_id=1, source_target_pairs={{0,1},{1,0},{2,3},{3,2},{4,5},{5,4},{6,7},{7,6},{8,9},{9,8},{10,11... | collective-permute-start | bytes 1769480 | tf_op jit(solution)/shard_map/ppermute | solution.py:227
  162.6 3.7 %collective-permute-start.12 = (bf16[192,1536]{1,0:T(8,128)(2,1)S(1)}, bf16[192,1536]{1,0:T(8,128)(2,1)}, u32[]{:S(2)}, u32[]{:S(2)}) collective-permute-start(bf16[192,1536]{1,0:T(8,128)(2,1)S(1)} %collective-permute-done.4.refs_3_), channel_id=1, source_target_pairs={{0,1},{1,0},{2,3},{3,2},{4,5},{5,4},{6,7},{7,6},{8,9},{9,8},{10,11... | collective-permute-start | bytes 1769480 | tf_op jit(solution)/shard_map/ppermute | solution.py:227
  166.4 6.6 %collective-permute-done.8.refs_7_ = bf16[192,1536]{1,0:T(8,128)(2,1)} collective-permute-done((bf16[192,1536]{1,0:T(8,128)(2,1)S(1)}, bf16[192,1536]{1,0:T(8,128)(2,1)}, u32[]{:S(2)}, u32[]{:S(2)}) %collective-permute-start.8) | collective-permute-done | bytes 589856 | tf_op jit(solution)/shard_map/ppermute | solution.py:227
  173.7 3.3 %merge.7.refs_19_ = bf16[384,384]{1,0:T(8,128)(2,1)} custom-call(s32[1]{0:T(128)} %bitcast.1.edge, f32[400,384]{1,0:T(8,128)} %get-tuple-element.26.own, bf16[400,384]{1,0:T(8,128)(2,1)} %copy-done.2, bf16[400,384]{1,0:T(8,128)(2,1)} %copy-done.3), custom_call_target="tpu_custom_call" | custom-call | flops 1179648 | bytes 1474560 | tf_op jit(solution)/shard_map/merge/pallas_call | solution.py:150
  177.0 3.3 %merge.6.refs_18_ = bf16[384,384]{1,0:T(8,128)(2,1)} custom-call(s32[1]{0:T(128)} %bitcast.1.edge, f32[400,384]{1,0:T(8,128)} %get-tuple-element.23.own, bf16[400,384]{1,0:T(8,128)(2,1)} %copy-done.4, bf16[400,384]{1,0:T(8,128)(2,1)} %copy-done.5), custom_call_target="tpu_custom_call" | custom-call | flops 1179648 | bytes 1474560 | tf_op jit(solution)/shard_map/merge/pallas_call | solution.py:150
  180.3 3.3 %merge.5.refs_17_ = bf16[384,384]{1,0:T(8,128)(2,1)} custom-call(s32[1]{0:T(128)} %bitcast.1.edge, f32[400,384]{1,0:T(8,128)} %get-tuple-element.20.own, bf16[400,384]{1,0:T(8,128)(2,1)} %copy-done.6, bf16[400,384]{1,0:T(8,128)(2,1)} %copy-done.7), custom_call_target="tpu_custom_call" | custom-call | flops 1179648 | bytes 1474560 | tf_op jit(solution)/shard_map/merge/pallas_call | solution.py:150
  183.7 3.3 %merge.4.refs_16_ = bf16[384,384]{1,0:T(8,128)(2,1)} custom-call(s32[1]{0:T(128)} %bitcast.1.edge, f32[400,384]{1,0:T(8,128)} %get-tuple-element.17.own, bf16[400,384]{1,0:T(8,128)(2,1)} %copy-done.8, bf16[400,384]{1,0:T(8,128)(2,1)} %copy-done.9), custom_call_target="tpu_custom_call" | custom-call | flops 1179648 | bytes 1474560 | tf_op jit(solution)/shard_map/merge/pallas_call | solution.py:150
  187.0 13.3 %project.1 = bf16[384,3072]{1,0:T(8,128)(2,1)} custom-call(bf16[192,1536]{1,0:T(8,128)(2,1)} %copy-done, bf16[192,1536]{1,0:T(8,128)(2,1)} %copy-done.1, bf16[192,1536]{1,0:T(8,128)(2,1)} %collective-permute-done.3.refs_2_, bf16[192,1536]{1,0:T(8,128)(2,1)} %copy-done.21, bf16[192,1536]{1,0:T(8,128)(2,1)} %collective-permute-done.5.refs_4_, ...), custom_call_target="tpu_custom_call" | custom-call | flops 3623878656 | bytes 9437184 | tf_op jit(solution)/shard_map/project/pallas_call | solution.py:211
  (106 shorter events, 36.4 us)
Async XLA Ops:
  3.5 20.6 %collective-permute-start.32 = (bf16[2,384,384]{2,1,0:T(8,128)(2,1)S(1)}, bf16[2,384,384]{2,1,0:T(8,128)(2,1)S(1)}, u32[]{:S(2)}, u32[]{:S(2)}) collective-permute-start(bf16[2,384,384]{2,1,0:T(8,128)(2,1)S(1)} %get-tuple-element.29), channel_id=1, source_target_pairs={{8,16},{16,8},{9,17},{17,9},{10,18},{18,10},{11,19},{19,11},{12,20... | collective-permute-start | bytes 1769480 | tf_op jit(solution)/shard_map/ppermute | solution.py:227
  6.8 26.6 %collective-permute-start.27 = (bf16[2,384,384]{2,1,0:T(8,128)(2,1)S(1)}, bf16[2,384,384]{2,1,0:T(8,128)(2,1)S(1)}, u32[]{:S(2)}, u32[]{:S(2)}) collective-permute-start(bf16[2,384,384]{2,1,0:T(8,128)(2,1)S(1)} %get-tuple-element.30), channel_id=1, source_target_pairs={{0,8},{8,0},{1,9},{9,1},{2,10},{10,2},{3,11},{11,3},{4,12},{12,4},... | collective-permute-start | bytes 1769480 | tf_op jit(solution)/shard_map/ppermute | solution.py:227
  6.9 29.7 %collective-permute-start.28 = (bf16[2,384,384]{2,1,0:T(8,128)(2,1)S(1)}, bf16[2,384,384]{2,1,0:T(8,128)(2,1)S(1)}, u32[]{:S(2)}, u32[]{:S(2)}) collective-permute-start(bf16[2,384,384]{2,1,0:T(8,128)(2,1)S(1)} %get-tuple-element.30), channel_id=1, source_target_pairs={{8,16},{16,8},{9,17},{17,9},{10,18},{18,10},{11,19},{19,11},{12,20... | collective-permute-start | bytes 1769480 | tf_op jit(solution)/shard_map/ppermute | solution.py:227
  8.8 37.2 %collective-permute-start.23 = (bf16[2,384,384]{2,1,0:T(8,128)(2,1)S(1)}, bf16[2,384,384]{2,1,0:T(8,128)(2,1)S(1)}, u32[]{:S(2)}, u32[]{:S(2)}) collective-permute-start(bf16[2,384,384]{2,1,0:T(8,128)(2,1)S(1)} %get-tuple-element.31), channel_id=1, source_target_pairs={{0,8},{8,0},{1,9},{9,1},{2,10},{10,2},{3,11},{11,3},{4,12},{12,4},... | collective-permute-start | bytes 1769480 | tf_op jit(solution)/shard_map/ppermute | solution.py:227
  20.7 28.5 %collective-permute-start.24 = (bf16[2,384,384]{2,1,0:T(8,128)(2,1)S(1)}, bf16[2,384,384]{2,1,0:T(8,128)(2,1)S(1)}, u32[]{:S(2)}, u32[]{:S(2)}) collective-permute-start(bf16[2,384,384]{2,1,0:T(8,128)(2,1)S(1)} %get-tuple-element.31), channel_id=1, source_target_pairs={{8,16},{16,8},{9,17},{17,9},{10,18},{18,10},{11,19},{19,11},{12,20... | collective-permute-start | bytes 1769480 | tf_op jit(solution)/shard_map/ppermute | solution.py:227
  24.0 34.7 %collective-permute-start.19 = (bf16[2,384,384]{2,1,0:T(8,128)(2,1)S(1)}, bf16[2,384,384]{2,1,0:T(8,128)(2,1)S(1)}, u32[]{:S(2)}, u32[]{:S(2)}) collective-permute-start(bf16[2,384,384]{2,1,0:T(8,128)(2,1)S(1)} %get-tuple-element.32), channel_id=1, source_target_pairs={{0,8},{8,0},{1,9},{9,1},{2,10},{10,2},{3,11},{11,3},{4,12},{12,4},... | collective-permute-start | bytes 1769480 | tf_op jit(solution)/shard_map/ppermute | solution.py:227
  33.4 26.6 %collective-permute-start.20 = (bf16[2,384,384]{2,1,0:T(8,128)(2,1)S(1)}, bf16[2,384,384]{2,1,0:T(8,128)(2,1)S(1)}, u32[]{:S(2)}, u32[]{:S(2)}) collective-permute-start(bf16[2,384,384]{2,1,0:T(8,128)(2,1)S(1)} %get-tuple-element.32), channel_id=1, source_target_pairs={{8,16},{16,8},{9,17},{17,9},{10,18},{18,10},{11,19},{19,11},{12,20... | collective-permute-start | bytes 1769480 | tf_op jit(solution)/shard_map/ppermute | solution.py:227
  36.6 58.1 %collective-permute-start.17 = (bf16[384,1536]{1,0:T(8,128)(2,1)S(1)}, bf16[384,1536]{1,0:T(8,128)(2,1)}, u32[]{:S(2)}, u32[]{:S(2)}) collective-permute-start(bf16[384,1536]{1,0:T(8,128)(2,1)S(1)} %bitcast.21), channel_id=1, source_target_pairs={{0,1},{1,0},{2,3},{3,2},{4,5},{5,4},{6,7},{7,6},{8,9},{9,8},{10,11... | collective-permute-start | bytes 3538952 | tf_op jit(solution)/shard_map/ppermute | solution.py:227
  46.0 23.6 %collective-permute-start.1 = (bf16[192,1536]{1,0:T(8,128)(2,1)S(1)}, bf16[192,1536]{1,0:T(8,128)(2,1)S(1)}, u32[]{:S(2)}, u32[]{:S(2)}) collective-permute-start(bf16[192,1536]{1,0:T(8,128)(2,1)S(1)} %pad_maximum_fusion.refs_0_), channel_id=1, source_target_pairs={{8,16},{16,8},{9,17},{17,9},{10,18},{18,10},{11,19},{19,11},{12,20... | collective-permute-start | bytes 1769480 | tf_op jit(solution)/shard_map/ppermute | solution.py:227
  49.2 46.4 %collective-permute-start.18 = (bf16[384,1536]{1,0:T(8,128)(2,1)S(1)}, bf16[384,1536]{1,0:T(8,128)(2,1)}, u32[]{:S(2)}, u32[]{:S(2)}) collective-permute-start(bf16[384,1536]{1,0:T(8,128)(2,1)S(1)} %bitcast.22), channel_id=1, source_target_pairs={{1,2},{2,1},{3,4},{4,3},{5,6},{6,5},{9,10},{10,9},{11,12},{12,11},... | collective-permute-start | bytes 3538952 | tf_op jit(solution)/shard_map/ppermute | solution.py:227
  58.8 33.9 %collective-permute-start.3 = (bf16[192,1536]{1,0:T(8,128)(2,1)S(1)}, bf16[192,1536]{1,0:T(8,128)(2,1)}, u32[]{:S(2)}, u32[]{:S(2)}) collective-permute-start(bf16[192,1536]{1,0:T(8,128)(2,1)S(1)} %pad_maximum_fusion.refs_0_), channel_id=1, source_target_pairs={{0,2},{1,3},{2,0},{3,1},{4,6},{5,7},{6,4},{7,5},{8,10},{9,11},{10,... | collective-permute-start | bytes 1769480 | tf_op jit(solution)/shard_map/ppermute | solution.py:227
  60.0 32.7 %collective-permute-start.5 = (bf16[192,1536]{1,0:T(8,128)(2,1)S(1)}, bf16[192,1536]{1,0:T(8,128)(2,1)}, u32[]{:S(2)}, u32[]{:S(2)}) collective-permute-start(bf16[192,1536]{1,0:T(8,128)(2,1)S(1)} %pad_maximum_fusion.refs_0_), channel_id=1, source_target_pairs={{0,4},{1,5},{2,6},{3,7},{4,0},{5,1},{6,2},{7,3},{8,12},{9,13},{10,... | collective-permute-start | bytes 1769480 | tf_op jit(solution)/shard_map/ppermute | solution.py:227
  69.7 25.8 %collective-permute-start.2 = (bf16[192,1536]{1,0:T(8,128)(2,1)S(1)}, bf16[192,1536]{1,0:T(8,128)(2,1)S(1)}, u32[]{:S(2)}, u32[]{:S(2)}) collective-permute-start(bf16[192,1536]{1,0:T(8,128)(2,1)S(1)} %collective-permute-done.1), channel_id=1, source_target_pairs={{8,0},{9,1},{10,2},{11,3},{12,4},{13,5},{14,6},{15,7},{16,24},{17,... | collective-permute-start | bytes 1769480 | tf_op jit(solution)/shard_map/ppermute | solution.py:227
  94.7 37.2 %collective-permute-start.11 = (bf16[192,1536]{1,0:T(8,128)(2,1)}, bf16[192,1536]{1,0:T(8,128)(2,1)}, u32[]{:S(2)}, u32[]{:S(2)}) collective-permute-start(bf16[192,1536]{1,0:T(8,128)(2,1)} %collective-permute-done.3.refs_2_), channel_id=1, source_target_pairs={{0,1},{1,0},{2,3},{3,2},{4,5},{5,4},{6,7},{7,6},{8,9},{9,8},{10,11... | collective-permute-start | bytes 1769480 | tf_op jit(solution)/shard_map/ppermute | solution.py:227
  95.5 36.5 %collective-permute-start.13 = (bf16[192,1536]{1,0:T(8,128)(2,1)}, bf16[192,1536]{1,0:T(8,128)(2,1)}, u32[]{:S(2)}, u32[]{:S(2)}) collective-permute-start(bf16[192,1536]{1,0:T(8,128)(2,1)} %collective-permute-done.5.refs_4_), channel_id=1, source_target_pairs={{0,1},{1,0},{2,3},{3,2},{4,5},{5,4},{6,7},{7,6},{8,9},{9,8},{10,11... | collective-permute-start | bytes 1769480 | tf_op jit(solution)/shard_map/ppermute | solution.py:227
  95.6 40.2 %collective-permute-start.4 = (bf16[192,1536]{1,0:T(8,128)(2,1)S(1)}, bf16[192,1536]{1,0:T(8,128)(2,1)S(1)}, u32[]{:S(2)}, u32[]{:S(2)}) collective-permute-start(bf16[192,1536]{1,0:T(8,128)(2,1)S(1)} %broadcast_select_fusion.refs_1_), channel_id=1, source_target_pairs={{0,2},{1,3},{2,0},{3,1},{4,6},{5,7},{6,4},{7,5},{8,10},{9,11},{10,... | collective-permute-start | bytes 1769480 | tf_op jit(solution)/shard_map/ppermute | solution.py:227
  105.4 28.8 %collective-permute-start.33 = (bf16[400,384]{1,0:T(8,128)(2,1)}, bf16[400,384]{1,0:T(8,128)(2,1)S(1)}, u32[]{:S(2)}, u32[]{:S(2)}) collective-permute-start(bf16[400,384]{1,0:T(8,128)(2,1)} %get-tuple-element.27), channel_id=1, source_target_pairs={{0,1},{1,0},{2,3},{3,2},{4,5},{5,4},{6,7},{7,6},{8,9},{9,8},{10,11... | collective-permute-start | bytes 921608 | tf_op jit(solution)/shard_map/ppermute | solution.py:227
  108.2 27.3 %collective-permute-start.34 = (bf16[400,384]{1,0:T(8,128)(2,1)}, bf16[400,384]{1,0:T(8,128)(2,1)S(1)}, u32[]{:S(2)}, u32[]{:S(2)}) collective-permute-start(bf16[400,384]{1,0:T(8,128)(2,1)} %get-tuple-element.28), channel_id=1, source_target_pairs={{1,2},{2,1},{3,4},{4,3},{5,6},{6,5},{9,10},{10,9},{11,12},{12,11},... | collective-permute-start | bytes 921608 | tf_op jit(solution)/shard_map/ppermute | solution.py:227
  135.5 30.8 %collective-permute-start.6 = (bf16[192,1536]{1,0:T(8,128)(2,1)S(1)}, bf16[192,1536]{1,0:T(8,128)(2,1)}, u32[]{:S(2)}, u32[]{:S(2)}) collective-permute-start(bf16[192,1536]{1,0:T(8,128)(2,1)S(1)} %broadcast_select_fusion.refs_1_), channel_id=1, source_target_pairs={{0,4},{1,5},{2,6},{3,7},{4,0},{5,1},{6,2},{7,3},{8,12},{9,13},{10,... | collective-permute-start | bytes 1769480 | tf_op jit(solution)/shard_map/ppermute | solution.py:227
  135.8 37.2 %collective-permute-start.8 = (bf16[192,1536]{1,0:T(8,128)(2,1)S(1)}, bf16[192,1536]{1,0:T(8,128)(2,1)}, u32[]{:S(2)}, u32[]{:S(2)}) collective-permute-start(bf16[192,1536]{1,0:T(8,128)(2,1)S(1)} %collective-permute-done.4.refs_3_), channel_id=1, source_target_pairs={{0,4},{1,5},{2,6},{3,7},{4,0},{5,1},{6,2},{7,3},{8,12},{9,13},{10,... | collective-permute-start | bytes 1769480 | tf_op jit(solution)/shard_map/ppermute | solution.py:227
  156.0 31.0 %collective-permute-start.10 = (bf16[192,1536]{1,0:T(8,128)(2,1)S(1)}, bf16[192,1536]{1,0:T(8,128)(2,1)}, u32[]{:S(2)}, u32[]{:S(2)}) collective-permute-start(bf16[192,1536]{1,0:T(8,128)(2,1)S(1)} %broadcast_select_fusion.refs_1_), channel_id=1, source_target_pairs={{0,1},{1,0},{2,3},{3,2},{4,5},{5,4},{6,7},{7,6},{8,9},{9,8},{10,11... | collective-permute-start | bytes 1769480 | tf_op jit(solution)/shard_map/ppermute | solution.py:227
  159.8 27.2 %collective-permute-start.15 = (bf16[192,1536]{1,0:T(8,128)(2,1)}, bf16[192,1536]{1,0:T(8,128)(2,1)}, u32[]{:S(2)}, u32[]{:S(2)}) collective-permute-start(bf16[192,1536]{1,0:T(8,128)(2,1)} %collective-permute-done.7.refs_6_), channel_id=1, source_target_pairs={{0,1},{1,0},{2,3},{3,2},{4,5},{5,4},{6,7},{7,6},{8,9},{9,8},{10,11... | collective-permute-start | bytes 1769480 | tf_op jit(solution)/shard_map/ppermute | solution.py:227
  162.6 24.4 %collective-permute-start.12 = (bf16[192,1536]{1,0:T(8,128)(2,1)S(1)}, bf16[192,1536]{1,0:T(8,128)(2,1)}, u32[]{:S(2)}, u32[]{:S(2)}) collective-permute-start(bf16[192,1536]{1,0:T(8,128)(2,1)S(1)} %collective-permute-done.4.refs_3_), channel_id=1, source_target_pairs={{0,1},{1,0},{2,3},{3,2},{4,5},{5,4},{6,7},{7,6},{8,9},{9,8},{10,11... | collective-permute-start | bytes 1769480 | tf_op jit(solution)/shard_map/ppermute | solution.py:227
  166.3 20.7 %collective-permute-start.14 = (bf16[192,1536]{1,0:T(8,128)(2,1)}, bf16[192,1536]{1,0:T(8,128)(2,1)}, u32[]{:S(2)}, u32[]{:S(2)}) collective-permute-start(bf16[192,1536]{1,0:T(8,128)(2,1)} %collective-permute-done.6.refs_5_), channel_id=1, source_target_pairs={{0,1},{1,0},{2,3},{3,2},{4,5},{5,4},{6,7},{7,6},{8,9},{9,8},{10,11... | collective-permute-start | bytes 1769480 | tf_op jit(solution)/shard_map/ppermute | solution.py:227
  (34 other events, 778.0 us)
where the time goes:
time: 201 us; the launch traced here: 200 us
  waiting for transfers between devices  73.8 us (37%)
  Pallas kernels  65.1 us (32%)
  starting transfers between devices  55.5 us (28%)
  local copies, waits for them, and re-layouts  2.66 us (1%)
  between operations  2.61 us (1%)
    ppermute x35, waiting for transfers between devices, passed(): return lax.ppermute(value, 'wa', pairs)  73.8 us
    ppermute x35, starting transfers between devices, passed(): return lax.ppermute(value, 'wa', pairs)  55.5 us
    pallas_call x4, Pallas kernels, attend(): pl.pallas_call(attend_kernel, grid_spec=pltpu.PrefetchScalarGridSpec(num_...  38.6 us
    pallas_call x4, Pallas kernels, merge(): pl.pallas_call(merge_kernel, grid_spec=pltpu.PrefetchScalarGridSpec(num_s...  13.3 us
    pallas_call x1, Pallas kernels, project(): pl.pallas_call(functools.partial(project_kernel, masks, shard, group, GW)...  13.3 us
  transfers between devices with their start and end apart: 35, of which 10 were waited for; matrix products, arithmetic and copies ran while one was open for 2% of the time, Pallas kernels for 26%

commit v1 on v0

v1 whole, which is shorter than its diff:
```python
import functools
import math

import jax
import jax.numpy as jnp
from jax import lax
from jax.experimental import pallas as pl
from jax.experimental.pallas import tpu as pltpu
from jax.sharding import PartitionSpec as P


HEAD_DIM = 128
GW = 8
SHARES = (4, 4, 4)
STAT_ROWS = 16
VMEM_LIMIT = 67043328
STEP_HEADS = 2
BIG = 1e30


def pair_swaps(count, stride, parity, block):
    pairs = []
    for device in range(count):
        position = (device // stride) % block
        if position % 2 == parity % 2 and position + 1 < block:
            pairs.append((device, device + stride))
            pairs.append((device + stride, device))
    return pairs


def split_three(value):
    high = value.astype(jnp.bfloat16).astype(jnp.float32)
    rest = value - high
    middle = rest.astype(jnp.bfloat16).astype(jnp.float32)
    return [high, middle, rest - middle]


def attend_kernel(time_tile, grid_rows, own_row, visible, *refs):
    queries, outs = refs[:3], refs[-3:]
    windows, before = (refs[3:4], None) if own_row else (refs[3:5], refs[5:8])
    tile = queries[0].shape[0]
    me = lax.axis_index("wa")
    row, col = me // GW, lax.rem(me, GW)

    def marked(parity):
        near = jnp.where(lax.rem(row, 2) == parity, row + 1, row - 1)
        inside = (near >= 0) & (near < grid_rows)
        return inside & (visible[jnp.clip(near, 0, grid_rows - 1) * GW + col, time_tile] == 1)

    near_seen = None if own_row else (marked(0), marked(1))
    own_seen = visible[me, time_tile] == 1
    factor = HEAD_DIM ** (-0.5) * math.log2(math.e)
    unit = HEAD_DIM + STAT_ROWS

    @functools.cache
    def window(h):
        cols = slice(h * HEAD_DIM, (h + 1) * HEAD_DIM)
        keys = jnp.concatenate([kv[0, :, cols] for kv in windows], axis=0)
        values = jnp.concatenate([kv[1, :, cols].T for kv in windows], axis=1)
        return keys, jnp.concatenate([values, jnp.ones((STAT_ROWS, values.shape[1]), values.dtype)], axis=0)

    def score(h, place):
        query = queries[place][:, h * HEAD_DIM : (h + 1) * HEAD_DIM]
        return lax.dot_general(window(h)[0], query, (((1,), (1,)), ((), ())), preferred_element_type=jnp.float32)

    def finish(h, place, scores):
        body, tail = slice(h * unit, h * unit + HEAD_DIM), slice(h * unit + HEAD_DIM, (h + 1) * unit)
        seen = near_seen if near_seen is not None else (place == 0 or own_seen,)
        parts = [scores[t * tile : (t + 1) * tile] for t in range(len(windows))]
        peaks = [
            jnp.where(seen[t], jnp.max(part, axis=0, keepdims=True) * factor, -BIG) for t, part in enumerate(parts)
        ]
        if before is not None:
            stat = before[place][tail, :].astype(jnp.float32)
            peaks.append(stat[0:1] + stat[1:2] + stat[2:3])
        peak = functools.reduce(jnp.maximum, peaks)
        weights = [jnp.exp2(part * factor - jnp.where(seen[t], peak, BIG)) for t, part in enumerate(parts)]
        low = jnp.concatenate([w.astype(jnp.bfloat16) for w in weights], axis=0)
        summed = jnp.dot(window(h)[1], low, preferred_element_type=jnp.float32)
        total = summed[HEAD_DIM : HEAD_DIM + 1]
        summed = summed[:HEAD_DIM]
        if before is not None:
            share = jnp.exp2(peaks[-1] - peak)
            total = total + share
            summed = summed + before[place][body, :].astype(jnp.float32) * share
        some = total > 0.0
        safe = jnp.where(some, total, 1.0)
        level = jnp.where(some, peak + jnp.log2(safe), -BIG)
        outs[place][body, :] = (summed * (1.0 / safe)).astype(jnp.bfloat16)
        stats = split_three(level) + [jnp.zeros((STAT_ROWS - 3, tile), jnp.float32)]
        outs[place][tail, :] = jnp.concatenate(stats, axis=0).astype(jnp.bfloat16)

    order = [(h, place) for h in range(queries[0].shape[1] // HEAD_DIM) for place in range(3)]
    ahead = score(*order[0])
    for n, item in enumerate(order):
        scores = ahead
        if n + 1 < len(order):
            ahead = score(*order[n + 1])
        finish(*item, scores)


def attend(visible, time_tile, grid_rows, queries, windows, before, first_head, heads):
    tile = queries[0].shape[0]
    unit = HEAD_DIM + STAT_ROWS
    pair_count = 3 * tile * tile * heads * len(windows)
    few = math.gcd(math.gcd(heads, first_head), STEP_HEADS)
    first = first_head // few
    width = few * HEAD_DIM
    return pl.pallas_call(
        functools.partial(attend_kernel, time_tile, grid_rows, len(windows) == 1),
        grid_spec=pltpu.PrefetchScalarGridSpec(
            num_scalar_prefetch=1,
            grid=(heads // few,),
            in_specs=[pl.BlockSpec((tile, width), lambda h, f: (0, first + h))] * 3
            + [pl.BlockSpec((2, tile, width), lambda h, f: (0, 0, h))] * len(windows)
            + [pl.BlockSpec((few * unit, tile), lambda h, f: (first + h, 0))] * len(before),
            out_specs=[pl.BlockSpec((few * unit, tile), lambda h, f: (h, 0))] * 3,
        ),
        out_shape=[jax.ShapeDtypeStruct((heads * unit, tile), jnp.bfloat16)] * 3,
        cost_estimate=pl.CostEstimate(
            flops=pair_count * HEAD_DIM * 4,
            transcendentals=pair_count,
            bytes_accessed=heads * HEAD_DIM * tile * 2 * (6 + 2 * len(windows) + len(before)),
        ),
        compiler_params=pltpu.CompilerParams(vmem_limit_bytes=VMEM_LIMIT),
        name="attend",
    )(visible, *queries, *windows, *before)


def merge_head(parts, base, alone):
    levels = []
    for part in parts:
        stat = part[base + HEAD_DIM : base + HEAD_DIM + STAT_ROWS, :].astype(jnp.float32)
        levels.append(stat[0:1] + stat[1:2] + stat[2:3])
    levels[2] = jnp.where(alone, -BIG, levels[2])
    top = jnp.maximum(jnp.maximum(levels[0], levels[1]), levels[2])
    shares = [jnp.exp2(level - top) for level in levels]
    scale = 1.0 / (shares[0] + shares[1] + shares[2])
    mixed = None
    for part, share in zip(parts, shares):
        term = part[base : base + HEAD_DIM, :].astype(jnp.float32) * (share * scale)
        mixed = term if mixed is None else mixed + term
    return mixed


def alone_in_pairs():
    col = lax.rem(lax.axis_index("wa"), GW)
    return (col == 0) | (col == GW - 1)


def merge_kernel(*refs):
    attended = refs[-1]
    alone = alone_in_pairs()
    unit = HEAD_DIM + STAT_ROWS
    first = 0
    for j in range(0, len(refs) - 1, 3):
        for h in range(refs[j].shape[0] // unit):
            mixed = merge_head(refs[j : j + 3], h * unit, alone)
            attended[:, (first + h) * HEAD_DIM : (first + h + 1) * HEAD_DIM] = mixed.T.astype(jnp.bfloat16)
        first += refs[j].shape[0] // unit


def merge(partial):
    heads = sum(p.shape[0] for p in partial[::3]) // (HEAD_DIM + STAT_ROWS)
    return pl.pallas_call(
        merge_kernel,
        out_shape=jax.ShapeDtypeStruct((partial[0].shape[1], heads * HEAD_DIM), jnp.bfloat16),
        compiler_params=pltpu.CompilerParams(vmem_limit_bytes=VMEM_LIMIT),
        cost_estimate=pl.CostEstimate(
            flops=heads * partial[0].size, transcendentals=0, bytes_accessed=8 * heads * HEAD_DIM * partial[0].shape[1]
        ),
        name="merge",
    )(*partial)


def project_kernel(masks, shard, group, *refs):
    count = len(masks)
    pieces = refs[:count]
    early, partial = refs[count], refs[count + 1 : count + 4]
    out_ref, held, parts, attended, weight_sem, part_sem = refs[-6:]
    step = pl.program_id(0)
    me = lax.axis_index("wa")
    row = me // GW
    flip = jnp.where((row == 0) | (row == 3), GW, 0)
    unit = HEAD_DIM + STAT_ROWS
    ready = early.shape[1]

    def move(ref, place, owner):
        target = pl.ds(pl.multiple_of(owner * shard, shard), shard)
        return pltpu.make_async_copy(ref.at[pl.ds(place * shard, shard)], held.at[target], weight_sem.at[owner])

    @pl.when(step == 0)
    def _():
        copies = [pltpu.make_async_copy(ref, parts.at[i], part_sem.at[i]) for i, ref in enumerate(partial)]
        copies.append(pltpu.make_async_copy(early, attended.at[:, pl.ds(0, ready)], part_sem.at[3]))
        for one in copies:
            one.start()
        for ref, mask in zip(pieces, masks):
            first = jnp.bitwise_xor(me, mask)
            if mask & (2 * GW):
                first = jnp.bitwise_xor(first, flip)
            for place in range(2):
                move(ref, place, jnp.bitwise_xor(first, place * GW)).start()
        for one in copies:
            one.wait()
        alone = alone_in_pairs()
        for h in range(parts.shape[1] // unit):
            mixed = merge_head([parts.at[i] for i in range(3)], h * unit, alone)
            start = ready + h * HEAD_DIM
            attended[:, start : start + HEAD_DIM] = mixed.T.astype(jnp.bfloat16)

    for i in range(group):
        move(pieces[0], 0, step * group + i).wait()
    columns = pl.ds(pl.multiple_of(step * (group * shard), 128), group * shard)
    out_ref[...] = lax.dot_general(
        attended[...], held[columns, :], (((1,), (1,)), ((), ())), preferred_element_type=jnp.float32
    ).astype(jnp.bfloat16)


def weight_group(shard):
    return 256 // math.gcd(256, shard)


def project(early, partial, pieces, masks, shard, count):
    tile = partial[0].shape[1]
    depth = pieces[0].shape[1]
    group = weight_group(shard)
    return pl.pallas_call(
        functools.partial(project_kernel, masks, shard, group),
        grid=(count // group,),
        in_specs=[pl.BlockSpec(memory_space=pl.ANY)] * (len(pieces) + 4),
        out_specs=pl.BlockSpec((tile, group * shard), lambda g: (0, g)),
        out_shape=jax.ShapeDtypeStruct((tile, count * shard), jnp.bfloat16),
        scratch_shapes=[
            pltpu.VMEM((count * shard, depth), jnp.bfloat16),
            pltpu.VMEM((3, *partial[0].shape), jnp.bfloat16),
            pltpu.VMEM((tile, depth), jnp.bfloat16),
            pltpu.SemaphoreType.DMA((count,)),
            pltpu.SemaphoreType.DMA((4,)),
        ],
        cost_estimate=pl.CostEstimate(
            flops=2 * tile * depth * count * shard, transcendentals=0, bytes_accessed=2 * depth * count * shard
        ),
        compiler_params=pltpu.CompilerParams(vmem_limit_bytes=VMEM_LIMIT),
        name="project",
    )(*pieces, early, *partial)


def passed(value, pairs):
    return lax.ppermute(value, "wa", pairs)


def gather_weight(own, count, row_even, row_odd, edge_row):
    def swap(value, bit):
        return passed(value, [(device, device ^ bit) for device in range(count)])

    ab = jnp.concatenate([own, passed(own, row_even)], axis=0)
    inner = passed(ab, row_odd)
    outer = passed(inner, [(d, d ^ GW) for d in range(count) if d // GW in (1, 2)])
    cd = jnp.where(edge_row, outer, inner)
    pieces = {"ab": ab, "cd": cd}
    masks = {"ab": 0, "cd": 3 * GW}
    for bit, mark in ((2, "x"), (4, "y"), (1, "c")):
        for name in list(pieces):
            pieces[mark + name] = swap(pieces[name], bit)
            masks[mark + name] = masks[name] ^ bit
    return list(pieces.values()), tuple(masks.values())


def use_pieces(count, shard):
    return count == 4 * GW and shard % 16 == 0 and count % weight_group(shard) == 0


def local(queries, keys_values, tile_visible, out_weight):
    count = lax.axis_size("wa")
    grid_rows = count // GW
    row = lax.axis_index("wa") // GW
    time_tiles, _, width = queries.shape[1:]
    shard = out_weight.shape[1]

    row_even, row_odd = (pair_swaps(count, GW, parity, grid_rows) for parity in (0, 1))
    col_even, col_odd = (pair_swaps(count, 1, parity, GW) for parity in (0, 1))

    spread = use_pieces(count, shard)
    if spread:
        pieces, masks = gather_weight(out_weight.T, count, row_even, row_odd, (row == 0) | (row == 3))
    else:
        whole = lax.all_gather(out_weight, "wa", axis=1, tiled=True)

    head_count = width // HEAD_DIM
    chunks = [round(head_count * share / sum(SHARES)) for share in SHARES[:-1]]
    chunks.append(head_count - sum(chunks))
    outputs = []
    for t in range(time_tiles):
        query = queries[0, t]
        kv_own = keys_values[:, 0, t]
        near_queries = [passed(query, col_even), passed(query, col_odd)]
        first = 0
        partial = []
        for heads in chunks:
            cut = kv_own[:, :, first * HEAD_DIM : (first + heads) * HEAD_DIM]
            kv_near = [passed(cut, row_even), passed(cut, row_odd)]
            partial.append((first, heads, kv_near))
            first += heads
        results = []
        near_queries = [query] + near_queries
        before = attend(tile_visible, t, grid_rows, near_queries, [kv_own], [], 0, head_count)
        for first, heads, kv_near in partial:
            own, even, odd = attend(
                tile_visible, t, grid_rows, near_queries, kv_near, before, first, heads
            )
            results += [own, passed(even, col_even), passed(odd, col_odd)]
        if spread:
            early = merge(results[:-3])
            outputs.append(project(early, results[-3:], pieces, masks, shard, count))
        else:
            outputs.append(jnp.dot(merge(results), whole, preferred_element_type=jnp.float32).astype(jnp.bfloat16))
    return jnp.stack(outputs)[None]


def solution(mesh):
    in_specs = (
        P(("groups", "wa"), None, None, None),
        P(None, ("groups", "wa"), None, None, None),
        P("groups", None),
        P(None, "wa"),
    )
    out_specs = P(("groups", "wa"), None, None, None)

    return jax.shard_map(local, mesh=mesh, in_specs=in_specs, out_specs=out_specs, check_vma=False)
```

time: 201 us -> 171 us (0.85)
  the two profiles are of different devices: /device:TPU:13 before, /device:TPU:11 now
where the time goes in v1:
time: 171 us; the launch traced here: 170 us
  waiting for transfers between devices  68.3 us (40%)
  Pallas kernels  51.9 us (30%)
  starting transfers between devices  41.4 us (24%)
  local copies, waits for them, and re-layouts  5.7 us (3%)
  other arithmetic  2.81 us (2%)
    ppermute x31, waiting for transfers between devices, passed(): return lax.ppermute(value, 'wa', pairs)  68.3 us
    ppermute x31, starting transfers between devices, passed(): return lax.ppermute(value, 'wa', pairs)  41.4 us
    pallas_call x4, Pallas kernels, attend(): pl.pallas_call(functools.partial(attend_kernel, time_tile, grid_rows, len...  38.2 us
    pallas_call x1, Pallas kernels, project(): pl.pallas_call(functools.partial(project_kernel, masks, shard, group), gr...  10.4 us
  transfers between devices with their start and end apart: 31, of which 7 were waited for; matrix products, arithmetic and copies ran while one was open for 2% of the time, Pallas kernels for 24%

profile of v1, /device:TPU:11, one launch (start us, length us, event | category | flops | bytes accessed | tf_op | source)
XLA Modules:
  0.0 170.4 jit_solution(4203036878795912632)
XLA Ops:
  0.0 2.9 %fusion = (bf16[2,384,512]{2,1,0:T(8,128)(2,1)}, bf16[2,384,512]{2,1,0:T(8,128)(2,1)S(1)}, bf16[2,384,512]{2,1,0:T(8,128)(2,1)S(1)}) fusion(bf16[2,384,1536]{2,1,0:T(8,128)(2,1)} %bitcast.10), kind=kLoop, calls=%fused_computation.2 | loop fusion | bytes 4718592 | tf_op jit(solution)/shard_map/slice | solution.py:301
  3.1 4.3 %collective-permute-start.24 = (bf16[2,384,512]{2,1,0:T(8,128)(2,1)S(1)}, bf16[2,384,512]{2,1,0:T(8,128)(2,1)S(1)}, u32[]{:S(2)}, u32[]{:S(2)}) collective-permute-start(bf16[2,384,512]{2,1,0:T(8,128)(2,1)S(1)} %get-tuple-element.30), channel_id=1, source_target_pairs={{8,16},{16,8},{9,17},{17,9},{10,18},{18,10},{11,19},{19,11},{12,20... | collective-permute-start | bytes 2359304 | tf_op jit(solution)/shard_map/ppermute | solution.py:250
  10.7 16.9 %collective-permute-done = bf16[96,1536]{1,0:T(8,128)(2,1)S(1)} collective-permute-done((bf16[96,1536]{1,0:T(8,128)(2,1)S(1)}, bf16[96,1536]{1,0:T(8,128)(2,1)S(1)}, u32[]{:S(2)}, u32[]{:S(2)}) %collective-permute-start) | collective-permute-done | bytes 294944 | tf_op jit(solution)/shard_map/ppermute | solution.py:250
  27.6 5.7 %collective-permute-start.18 = (bf16[384,1536]{1,0:T(8,128)(2,1)S(1)}, bf16[384,1536]{1,0:T(8,128)(2,1)S(1)}, u32[]{:S(2)}, u32[]{:S(2)}) collective-permute-start(bf16[384,1536]{1,0:T(8,128)(2,1)S(1)} %bitcast.9), channel_id=1, source_target_pairs={{1,2},{2,1},{3,4},{4,3},{5,6},{6,5},{9,10},{10,9},{11,12},{12,11},... | collective-permute-start | bytes 3538952 | tf_op jit(solution)/shard_map/ppermute | solution.py:250
  33.3 3.2 %collective-permute-start.20 = (bf16[2,384,512]{2,1,0:T(8,128)(2,1)S(1)}, bf16[2,384,512]{2,1,0:T(8,128)(2,1)S(1)}, u32[]{:S(2)}, u32[]{:S(2)}) collective-permute-start(bf16[2,384,512]{2,1,0:T(8,128)(2,1)S(1)} %get-tuple-element.31), channel_id=1, source_target_pairs={{8,16},{16,8},{9,17},{17,9},{10,18},{18,10},{11,19},{19,11},{12,20... | collective-permute-start | bytes 2359304 | tf_op jit(solution)/shard_map/ppermute | solution.py:250
  37.4 2.1 %collective-permute-start.1 = (bf16[192,1536]{1,0:T(8,128)(2,1)}, bf16[192,1536]{1,0:T(8,128)(2,1)}, u32[]{:S(2)}, u32[]{:S(2)}) collective-permute-start(bf16[192,1536]{1,0:T(8,128)(2,1)} %pad_maximum_fusion.refs_0_), channel_id=1, source_target_pairs={{8,16},{16,8},{9,17},{17,9},{10,18},{18,10},{11,19},{19,11},{12,20... | collective-permute-start | bytes 1769480 | tf_op jit(solution)/shard_map/ppermute | solution.py:250
  39.5 5.0 %collective-permute-done.19.refs_3_ = bf16[2,384,512]{2,1,0:T(8,128)(2,1)S(1)} collective-permute-done((bf16[2,384,512]{2,1,0:T(8,128)(2,1)S(1)}, bf16[2,384,512]{2,1,0:T(8,128)(2,1)S(1)}, u32[]{:S(2)}, u32[]{:S(2)}) %collective-permute-start.19) | collective-permute-done | bytes 786464 | tf_op jit(solution)/shard_map/ppermute | solution.py:250
  44.7 10.2 %collective-permute-done.20.refs_4_ = bf16[2,384,512]{2,1,0:T(8,128)(2,1)S(1)} collective-permute-done((bf16[2,384,512]{2,1,0:T(8,128)(2,1)S(1)}, bf16[2,384,512]{2,1,0:T(8,128)(2,1)S(1)}, u32[]{:S(2)}, u32[]{:S(2)}) %collective-permute-start.20) | collective-permute-done | bytes 786464 | tf_op jit(solution)/shard_map/ppermute | solution.py:250
  55.1 11.8 %collective-permute-done.1 = bf16[192,1536]{1,0:T(8,128)(2,1)} collective-permute-done((bf16[192,1536]{1,0:T(8,128)(2,1)}, bf16[192,1536]{1,0:T(8,128)(2,1)}, u32[]{:S(2)}, u32[]{:S(2)}) %collective-permute-start.1) | collective-permute-done | bytes 589856 | tf_op jit(solution)/shard_map/ppermute | solution.py:250
  66.9 2.1 %collective-permute-start.2 = (bf16[192,1536]{1,0:T(8,128)(2,1)}, bf16[192,1536]{1,0:T(8,128)(2,1)}, u32[]{:S(2)}, u32[]{:S(2)}) collective-permute-start(bf16[192,1536]{1,0:T(8,128)(2,1)} %collective-permute-done.1), channel_id=1, source_target_pairs={{8,0},{9,1},{10,2},{11,3},{12,4},{13,5},{14,6},{15,7},{16,24},{17,... | collective-permute-start | bytes 1769480 | tf_op jit(solution)/shard_map/ppermute | solution.py:250
  70.1 3.2 %collective-permute-start.28 = (bf16[2,384,512]{2,1,0:T(8,128)(2,1)}, bf16[2,384,512]{2,1,0:T(8,128)(2,1)}, u32[]{:S(2)}, u32[]{:S(2)}) collective-permute-start(bf16[2,384,512]{2,1,0:T(8,128)(2,1)} %get-tuple-element.29), channel_id=1, source_target_pairs={{8,16},{16,8},{9,17},{17,9},{10,18},{18,10},{11,19},{19,11},{12,20... | collective-permute-start | bytes 2359304 | tf_op jit(solution)/shard_map/ppermute | solution.py:250
  75.1 12.9 %attend.4 = (bf16[1728,384]{1,0:T(8,128)(2,1)}, bf16[1728,384]{1,0:T(8,128)(2,1)}, bf16[1728,384]{1,0:T(8,128)(2,1)}) custom-call(s32[32,1]{1,0:T(8,128)} %copy.6.visible, bf16[384,1536]{1,0:T(8,128)(2,1)} %bitcast.4, bf16[384,1536]{1,0:T(8,128)(2,1)} %copy-done.1, bf16[384,1536]{1,0:T(8,128)(2,1)} %copy-done.2, bf16[2,384,1536]{2,1,0:T(8,128)(2,1)} %bitcast.11), custom_call_target="tpu_custom_call" | custom-call | flops 2717908992 | bytes 9437184 | tf_op jit(solution)/shard_map/attend/pallas_call | solution.py:109
  90.3 1.9 %broadcast_select_fusion.refs_1_ = bf16[192,1536]{1,0:T(8,128)(2,1)} fusion(bf16[192,1536]{1,0:T(8,128)(2,1)} %collective-permute-done.2, bf16[192,1536]{1,0:T(8,128)(2,1)} %collective-permute-done.1, pred[]{:T(512)S(6)} %or.3), kind=kLoop, calls=%fused_computation.1 | loop fusion | flops 294912 | bytes 1769473 | tf_op jit(solution)/shard_map/jit(_where)/select_n | solution.py:260
  92.4 8.4 %attend.6 = (bf16[576,384]{1,0:T(8,128)(2,1)}, bf16[576,384]{1,0:T(8,128)(2,1)}, bf16[576,384]{1,0:T(8,128)(2,1)}) custom-call(s32[32,1]{1,0:T(8,128)} %copy.6.visible, bf16[384,1536]{1,0:T(8,128)(2,1)} %bitcast.5, bf16[384,1536]{1,0:T(8,128)(2,1)} %copy-done.1, bf16[384,1536]{1,0:T(8,128)(2,1)} %copy-done.2, ...), custom_call_target="tpu_custom_call" | custom-call | flops 1811939328 | bytes 5111808 | tf_op jit(solution)/shard_map/attend/pallas_call | solution.py:109
  100.9 8.4 %attend.5 = (bf16[576,384]{1,0:T(8,128)(2,1)}, bf16[576,384]{1,0:T(8,128)(2,1)}, bf16[576,384]{1,0:T(8,128)(2,1)}) custom-call(s32[32,1]{1,0:T(8,128)} %copy.6.visible, bf16[384,1536]{1,0:T(8,128)(2,1)} %bitcast.6, bf16[384,1536]{1,0:T(8,128)(2,1)} %copy-done.1, bf16[384,1536]{1,0:T(8,128)(2,1)} %copy-done.2, bf16[2,384,512]{2,1,0:T(8,128)(2,1)} %copy-done.4, ...), custom_call_target="tpu_custom_call" | custom-call | flops 1811939328 | bytes 5111808 | tf_op jit(solution)/shard_map/attend/pallas_call | solution.py:109
  110.0 3.0 %collective-permute-start.26 = (bf16[576,384]{1,0:T(8,128)(2,1)}, bf16[576,384]{1,0:T(8,128)(2,1)}, u32[]{:S(2)}, u32[]{:S(2)}) collective-permute-start(bf16[576,384]{1,0:T(8,128)(2,1)} %get-tuple-element.25), channel_id=1, source_target_pairs={{1,2},{2,1},{3,4},{4,3},{5,6},{6,5},{9,10},{10,9},{11,12},{12,11},... | collective-permute-start | bytes 1327112 | tf_op jit(solution)/shard_map/ppermute | solution.py:250
  115.3 8.5 %attend.7 = (bf16[576,384]{1,0:T(8,128)(2,1)}, bf16[576,384]{1,0:T(8,128)(2,1)}, bf16[576,384]{1,0:T(8,128)(2,1)}) custom-call(s32[32,1]{1,0:T(8,128)} %copy.6.visible, bf16[384,1536]{1,0:T(8,128)(2,1)} %bitcast.7, bf16[384,1536]{1,0:T(8,128)(2,1)} %copy-done.1, bf16[384,1536]{1,0:T(8,128)(2,1)} %copy-done.2, ...), custom_call_target="tpu_custom_call" | custom-call | flops 1811939328 | bytes 5111808 | tf_op jit(solution)/shard_map/attend/pallas_call | solution.py:109
  123.8 3.6 %collective-permute-start.22 = (bf16[576,384]{1,0:T(8,128)(2,1)}, bf16[576,384]{1,0:T(8,128)(2,1)}, u32[]{:S(2)}, u32[]{:S(2)}) collective-permute-start(bf16[576,384]{1,0:T(8,128)(2,1)} %get-tuple-element.22), channel_id=1, source_target_pairs={{1,2},{2,1},{3,4},{4,3},{5,6},{6,5},{9,10},{10,9},{11,12},{12,11},... | collective-permute-start | bytes 1327112 | tf_op jit(solution)/shard_map/ppermute | solution.py:250
  127.5 3.1 %collective-permute-start.30 = (bf16[576,384]{1,0:T(8,128)(2,1)}, bf16[576,384]{1,0:T(8,128)(2,1)}, u32[]{:S(2)}, u32[]{:S(2)}) collective-permute-start(bf16[576,384]{1,0:T(8,128)(2,1)} %get-tuple-element.28), channel_id=1, source_target_pairs={{1,2},{2,1},{3,4},{4,3},{5,6},{6,5},{9,10},{10,9},{11,12},{12,11},... | collective-permute-start | bytes 1327112 | tf_op jit(solution)/shard_map/ppermute | solution.py:250
  130.6 8.8 %collective-permute-done.22.refs_2_ = bf16[576,384]{1,0:T(8,128)(2,1)} collective-permute-done((bf16[576,384]{1,0:T(8,128)(2,1)}, bf16[576,384]{1,0:T(8,128)(2,1)}, u32[]{:S(2)}, u32[]{:S(2)}) %collective-permute-start.22) | collective-permute-done | bytes 442400 | tf_op jit(solution)/shard_map/ppermute | solution.py:250
  139.9 7.8 %collective-permute-done.30.refs_19_ = bf16[576,384]{1,0:T(8,128)(2,1)} collective-permute-done((bf16[576,384]{1,0:T(8,128)(2,1)}, bf16[576,384]{1,0:T(8,128)(2,1)}, u32[]{:S(2)}, u32[]{:S(2)}) %collective-permute-start.30) | collective-permute-done | bytes 442400 | tf_op jit(solution)/shard_map/ppermute | solution.py:250
  148.3 7.6 %collective-permute-done.8.refs_7_ = bf16[192,1536]{1,0:T(8,128)(2,1)} collective-permute-done((bf16[192,1536]{1,0:T(8,128)(2,1)}, bf16[192,1536]{1,0:T(8,128)(2,1)}, u32[]{:S(2)}, u32[]{:S(2)}) %collective-permute-start.8) | collective-permute-done | bytes 589856 | tf_op jit(solution)/shard_map/ppermute | solution.py:250
  156.6 3.3 %merge.1.refs_16_ = bf16[384,1024]{1,0:T(8,128)(2,1)} custom-call(bf16[576,384]{1,0:T(8,128)(2,1)} %get-tuple-element.20.refs_0_, bf16[576,384]{1,0:T(8,128)(2,1)} %collective-permute-done.21.refs_1_, bf16[576,384]{1,0:T(8,128)(2,1)} %collective-permute-done.22.refs_2_, bf16[576,384]{1,0:T(8,128)(2,1)} %get-tuple-element.23.refs_3_, ...), custom_call_target="tpu_custom_call" | custom-call | flops 1769472 | bytes 3145728 | tf_op jit(solution)/shard_map/merge/pallas_call | solution.py:165
  159.9 10.4 %project.1 = bf16[384,3072]{1,0:T(8,128)(2,1)} custom-call(bf16[192,1536]{1,0:T(8,128)(2,1)} %pad_maximum_fusion.refs_0_, bf16[192,1536]{1,0:T(8,128)(2,1)} %broadcast_select_fusion.refs_1_, bf16[192,1536]{1,0:T(8,128)(2,1)} %collective-permute-done.3.refs_2_, bf16[192,1536]{1,0:T(8,128)(2,1)} %collective-permute-done.4.refs_3_, ...), custom_call_target="tpu_custom_call" | custom-call | flops 3623878656 | bytes 9437184 | tf_op jit(solution)/shard_map/project/pallas_call | solution.py:228
  (64 shorter events, 14.9 us)
Async XLA Ops:
  2.9 30.4 %collective-permute-start.23 = (bf16[2,384,512]{2,1,0:T(8,128)(2,1)S(1)}, bf16[2,384,512]{2,1,0:T(8,128)(2,1)}, u32[]{:S(2)}, u32[]{:S(2)}) collective-permute-start(bf16[2,384,512]{2,1,0:T(8,128)(2,1)S(1)} %get-tuple-element.30), channel_id=1, source_target_pairs={{0,8},{8,0},{1,9},{9,1},{2,10},{10,2},{3,11},{11,3},{4,12},{12,4},... | collective-permute-start | bytes 2359304 | tf_op jit(solution)/shard_map/ppermute | solution.py:250
  3.1 34.3 %collective-permute-start.24 = (bf16[2,384,512]{2,1,0:T(8,128)(2,1)S(1)}, bf16[2,384,512]{2,1,0:T(8,128)(2,1)S(1)}, u32[]{:S(2)}, u32[]{:S(2)}) collective-permute-start(bf16[2,384,512]{2,1,0:T(8,128)(2,1)S(1)} %get-tuple-element.30), channel_id=1, source_target_pairs={{8,16},{16,8},{9,17},{17,9},{10,18},{18,10},{11,19},{19,11},{12,20... | collective-permute-start | bytes 2359304 | tf_op jit(solution)/shard_map/ppermute | solution.py:250
  7.4 20.2 %collective-permute-start = (bf16[96,1536]{1,0:T(8,128)(2,1)S(1)}, bf16[96,1536]{1,0:T(8,128)(2,1)S(1)}, u32[]{:S(2)}, u32[]{:S(2)}) collective-permute-start(bf16[96,1536]{1,0:T(8,128)(2,1)S(1)} %bitcast.12), channel_id=1, source_target_pairs={{0,8},{8,0},{1,9},{9,1},{2,10},{10,2},{3,11},{11,3},{4,12},{12,4},... | collective-permute-start | bytes 884744 | tf_op jit(solution)/shard_map/ppermute | solution.py:250
  7.5 37.0 %collective-permute-start.19 = (bf16[2,384,512]{2,1,0:T(8,128)(2,1)S(1)}, bf16[2,384,512]{2,1,0:T(8,128)(2,1)S(1)}, u32[]{:S(2)}, u32[]{:S(2)}) collective-permute-start(bf16[2,384,512]{2,1,0:T(8,128)(2,1)S(1)} %get-tuple-element.31), channel_id=1, source_target_pairs={{0,8},{8,0},{1,9},{9,1},{2,10},{10,2},{3,11},{11,3},{4,12},{12,4},... | collective-permute-start | bytes 2359304 | tf_op jit(solution)/shard_map/ppermute | solution.py:250
  8.9 60.1 %collective-permute-start.17 = (bf16[384,1536]{1,0:T(8,128)(2,1)S(1)}, bf16[384,1536]{1,0:T(8,128)(2,1)S(1)}, u32[]{:S(2)}, u32[]{:S(2)}) collective-permute-start(bf16[384,1536]{1,0:T(8,128)(2,1)S(1)} %bitcast.8), channel_id=1, source_target_pairs={{0,1},{1,0},{2,3},{3,2},{4,5},{5,4},{6,7},{7,6},{8,9},{9,8},{10,11... | collective-permute-start | bytes 3538952 | tf_op jit(solution)/shard_map/ppermute | solution.py:250
  27.6 46.4 %collective-permute-start.18 = (bf16[384,1536]{1,0:T(8,128)(2,1)S(1)}, bf16[384,1536]{1,0:T(8,128)(2,1)S(1)}, u32[]{:S(2)}, u32[]{:S(2)}) collective-permute-start(bf16[384,1536]{1,0:T(8,128)(2,1)S(1)} %bitcast.9), channel_id=1, source_target_pairs={{1,2},{2,1},{3,4},{4,3},{5,6},{6,5},{9,10},{10,9},{11,12},{12,11},... | collective-permute-start | bytes 3538952 | tf_op jit(solution)/shard_map/ppermute | solution.py:250
  33.3 21.6 %collective-permute-start.20 = (bf16[2,384,512]{2,1,0:T(8,128)(2,1)S(1)}, bf16[2,384,512]{2,1,0:T(8,128)(2,1)S(1)}, u32[]{:S(2)}, u32[]{:S(2)}) collective-permute-start(bf16[2,384,512]{2,1,0:T(8,128)(2,1)S(1)} %get-tuple-element.31), channel_id=1, source_target_pairs={{8,16},{16,8},{9,17},{17,9},{10,18},{18,10},{11,19},{19,11},{12,20... | collective-permute-start | bytes 2359304 | tf_op jit(solution)/shard_map/ppermute | solution.py:250
  37.4 29.5 %collective-permute-start.1 = (bf16[192,1536]{1,0:T(8,128)(2,1)}, bf16[192,1536]{1,0:T(8,128)(2,1)}, u32[]{:S(2)}, u32[]{:S(2)}) collective-permute-start(bf16[192,1536]{1,0:T(8,128)(2,1)} %pad_maximum_fusion.refs_0_), channel_id=1, source_target_pairs={{8,16},{16,8},{9,17},{17,9},{10,18},{18,10},{11,19},{19,11},{12,20... | collective-permute-start | bytes 1769480 | tf_op jit(solution)/shard_map/ppermute | solution.py:250
  44.5 43.5 %collective-permute-start.27 = (bf16[2,384,512]{2,1,0:T(8,128)(2,1)}, bf16[2,384,512]{2,1,0:T(8,128)(2,1)}, u32[]{:S(2)}, u32[]{:S(2)}) collective-permute-start(bf16[2,384,512]{2,1,0:T(8,128)(2,1)} %get-tuple-element.29), channel_id=1, source_target_pairs={{0,8},{8,0},{1,9},{9,1},{2,10},{10,2},{3,11},{11,3},{4,12},{12,4},... | collective-permute-start | bytes 2359304 | tf_op jit(solution)/shard_map/ppermute | solution.py:250
  54.9 33.2 %collective-permute-start.3 = (bf16[192,1536]{1,0:T(8,128)(2,1)}, bf16[192,1536]{1,0:T(8,128)(2,1)}, u32[]{:S(2)}, u32[]{:S(2)}) collective-permute-start(bf16[192,1536]{1,0:T(8,128)(2,1)} %pad_maximum_fusion.refs_0_), channel_id=1, source_target_pairs={{0,2},{1,3},{2,0},{3,1},{4,6},{5,7},{6,4},{7,5},{8,10},{9,11},{10,... | collective-permute-start | bytes 1769480 | tf_op jit(solution)/shard_map/ppermute | solution.py:250
  66.9 23.0 %collective-permute-start.2 = (bf16[192,1536]{1,0:T(8,128)(2,1)}, bf16[192,1536]{1,0:T(8,128)(2,1)}, u32[]{:S(2)}, u32[]{:S(2)}) collective-permute-start(bf16[192,1536]{1,0:T(8,128)(2,1)} %collective-permute-done.1), channel_id=1, source_target_pairs={{8,0},{9,1},{10,2},{11,3},{12,4},{13,5},{14,6},{15,7},{16,24},{17,... | collective-permute-start | bytes 1769480 | tf_op jit(solution)/shard_map/ppermute | solution.py:250
  70.1 22.2 %collective-permute-start.28 = (bf16[2,384,512]{2,1,0:T(8,128)(2,1)}, bf16[2,384,512]{2,1,0:T(8,128)(2,1)}, u32[]{:S(2)}, u32[]{:S(2)}) collective-permute-start(bf16[2,384,512]{2,1,0:T(8,128)(2,1)} %get-tuple-element.29), channel_id=1, source_target_pairs={{8,16},{16,8},{9,17},{17,9},{10,18},{18,10},{11,19},{19,11},{12,20... | collective-permute-start | bytes 2359304 | tf_op jit(solution)/shard_map/ppermute | solution.py:250
  75.1 17.2 %collective-permute-start.5 = (bf16[192,1536]{1,0:T(8,128)(2,1)}, bf16[192,1536]{1,0:T(8,128)(2,1)}, u32[]{:S(2)}, u32[]{:S(2)}) collective-permute-start(bf16[192,1536]{1,0:T(8,128)(2,1)} %pad_maximum_fusion.refs_0_), channel_id=1, source_target_pairs={{0,4},{1,5},{2,6},{3,7},{4,0},{5,1},{6,2},{7,3},{8,12},{9,13},{10,... | collective-permute-start | bytes 1769480 | tf_op jit(solution)/shard_map/ppermute | solution.py:250
  88.0 21.3 %collective-permute-start.9 = (bf16[192,1536]{1,0:T(8,128)(2,1)}, bf16[192,1536]{1,0:T(8,128)(2,1)}, u32[]{:S(2)}, u32[]{:S(2)}) collective-permute-start(bf16[192,1536]{1,0:T(8,128)(2,1)} %pad_maximum_fusion.refs_0_), channel_id=1, source_target_pairs={{0,1},{1,0},{2,3},{3,2},{4,5},{5,4},{6,7},{7,6},{8,9},{9,8},{10,11... | collective-permute-start | bytes 1769480 | tf_op jit(solution)/shard_map/ppermute | solution.py:250
  88.1 21.9 %collective-permute-start.7 = (bf16[192,1536]{1,0:T(8,128)(2,1)}, bf16[192,1536]{1,0:T(8,128)(2,1)}, u32[]{:S(2)}, u32[]{:S(2)}) collective-permute-start(bf16[192,1536]{1,0:T(8,128)(2,1)} %collective-permute-done.3.refs_2_), channel_id=1, source_target_pairs={{0,4},{1,5},{2,6},{3,7},{4,0},{5,1},{6,2},{7,3},{8,12},{9,13},{10,... | collective-permute-start | bytes 1769480 | tf_op jit(solution)/shard_map/ppermute | solution.py:250
  89.9 23.2 %collective-permute-start.11 = (bf16[192,1536]{1,0:T(8,128)(2,1)}, bf16[192,1536]{1,0:T(8,128)(2,1)}, u32[]{:S(2)}, u32[]{:S(2)}) collective-permute-start(bf16[192,1536]{1,0:T(8,128)(2,1)} %collective-permute-done.3.refs_2_), channel_id=1, source_target_pairs={{0,1},{1,0},{2,3},{3,2},{4,5},{5,4},{6,7},{7,6},{8,9},{9,8},{10,11... | collective-permute-start | bytes 1769480 | tf_op jit(solution)/shard_map/ppermute | solution.py:250
  92.3 21.6 %collective-permute-start.13 = (bf16[192,1536]{1,0:T(8,128)(2,1)}, bf16[192,1536]{1,0:T(8,128)(2,1)}, u32[]{:S(2)}, u32[]{:S(2)}) collective-permute-start(bf16[192,1536]{1,0:T(8,128)(2,1)} %collective-permute-done.5.refs_4_), channel_id=1, source_target_pairs={{0,1},{1,0},{2,3},{3,2},{4,5},{5,4},{6,7},{7,6},{8,9},{9,8},{10,11... | collective-permute-start | bytes 1769480 | tf_op jit(solution)/shard_map/ppermute | solution.py:250
  92.3 21.6 %collective-permute-start.4 = (bf16[192,1536]{1,0:T(8,128)(2,1)}, bf16[192,1536]{1,0:T(8,128)(2,1)}, u32[]{:S(2)}, u32[]{:S(2)}) collective-permute-start(bf16[192,1536]{1,0:T(8,128)(2,1)} %broadcast_select_fusion.refs_1_), channel_id=1, source_target_pairs={{0,2},{1,3},{2,0},{3,1},{4,6},{5,7},{6,4},{7,5},{8,10},{9,11},{10,... | collective-permute-start | bytes 1769480 | tf_op jit(solution)/shard_map/ppermute | solution.py:250
  110.0 17.3 %collective-permute-start.26 = (bf16[576,384]{1,0:T(8,128)(2,1)}, bf16[576,384]{1,0:T(8,128)(2,1)}, u32[]{:S(2)}, u32[]{:S(2)}) collective-permute-start(bf16[576,384]{1,0:T(8,128)(2,1)} %get-tuple-element.25), channel_id=1, source_target_pairs={{1,2},{2,1},{3,4},{4,3},{5,6},{6,5},{9,10},{10,9},{11,12},{12,11},... | collective-permute-start | bytes 1327112 | tf_op jit(solution)/shard_map/ppermute | solution.py:250
  113.9 33.9 %collective-permute-start.6 = (bf16[192,1536]{1,0:T(8,128)(2,1)}, bf16[192,1536]{1,0:T(8,128)(2,1)}, u32[]{:S(2)}, u32[]{:S(2)}) collective-permute-start(bf16[192,1536]{1,0:T(8,128)(2,1)} %broadcast_select_fusion.refs_1_), channel_id=1, source_target_pairs={{0,4},{1,5},{2,6},{3,7},{4,0},{5,1},{6,2},{7,3},{8,12},{9,13},{10,... | collective-permute-start | bytes 1769480 | tf_op jit(solution)/shard_map/ppermute | solution.py:250
  113.9 42.0 %collective-permute-start.8 = (bf16[192,1536]{1,0:T(8,128)(2,1)}, bf16[192,1536]{1,0:T(8,128)(2,1)}, u32[]{:S(2)}, u32[]{:S(2)}) collective-permute-start(bf16[192,1536]{1,0:T(8,128)(2,1)} %collective-permute-done.4.refs_3_), channel_id=1, source_target_pairs={{0,4},{1,5},{2,6},{3,7},{4,0},{5,1},{6,2},{7,3},{8,12},{9,13},{10,... | collective-permute-start | bytes 1769480 | tf_op jit(solution)/shard_map/ppermute | solution.py:250
  127.5 20.2 %collective-permute-start.30 = (bf16[576,384]{1,0:T(8,128)(2,1)}, bf16[576,384]{1,0:T(8,128)(2,1)}, u32[]{:S(2)}, u32[]{:S(2)}) collective-permute-start(bf16[576,384]{1,0:T(8,128)(2,1)} %get-tuple-element.28), channel_id=1, source_target_pairs={{1,2},{2,1},{3,4},{4,3},{5,6},{6,5},{9,10},{10,9},{11,12},{12,11},... | collective-permute-start | bytes 1327112 | tf_op jit(solution)/shard_map/ppermute | solution.py:250
  139.4 20.5 %collective-permute-start.10 = (bf16[192,1536]{1,0:T(8,128)(2,1)}, bf16[192,1536]{1,0:T(8,128)(2,1)}, u32[]{:S(2)}, u32[]{:S(2)}) collective-permute-start(bf16[192,1536]{1,0:T(8,128)(2,1)} %broadcast_select_fusion.refs_1_), channel_id=1, source_target_pairs={{0,1},{1,0},{2,3},{3,2},{4,5},{5,4},{6,7},{7,6},{8,9},{9,8},{10,11... | collective-permute-start | bytes 1769480 | tf_op jit(solution)/shard_map/ppermute | solution.py:250
  139.4 20.5 %collective-permute-start.15 = (bf16[192,1536]{1,0:T(8,128)(2,1)}, bf16[192,1536]{1,0:T(8,128)(2,1)}, u32[]{:S(2)}, u32[]{:S(2)}) collective-permute-start(bf16[192,1536]{1,0:T(8,128)(2,1)} %collective-permute-done.7.refs_6_), channel_id=1, source_target_pairs={{0,1},{1,0},{2,3},{3,2},{4,5},{5,4},{6,7},{7,6},{8,9},{9,8},{10,11... | collective-permute-start | bytes 1769480 | tf_op jit(solution)/shard_map/ppermute | solution.py:250
  (15 other events, 259.7 us)

commit v2 on v1

--- a/solution.py
+++ b/solution.py
@@ -11,9 +11,9 @@
 
 HEAD_DIM = 128
 GW = 8
-SHARES = (4, 4, 4)
-STAT_ROWS = 16
-VMEM_LIMIT = 67043328
+SHARES = (6, 4, 2)
+STAT_ROWS = 8
+VMEM_LIMIT = 23068672
 STEP_HEADS = 2
 BIG = 1e30
 

time: 171 us -> 181 us (1.058)
  the two profiles are of different devices: /device:TPU:11 before, /device:TPU:7 now
where the time goes in v2:
time: 181 us; the launch traced here: 179 us
  starting transfers between devices  78.6 us (43%)
  waiting for transfers between devices  47.9 us (26%)
  Pallas kernels  40.2 us (22%)
  local copies, waits for them, and re-layouts  8.4 us (5%)
  other arithmetic  2.97 us (2%)
    ppermute x31, starting transfers between devices, passed(): return lax.ppermute(value, 'wa', pairs)  78.6 us
    ppermute x31, waiting for transfers between devices, passed(): return lax.ppermute(value, 'wa', pairs)  47.9 us
    pallas_call x4, Pallas kernels, attend(): pl.pallas_call(functools.partial(attend_kernel, time_tile, grid_rows, len...  30.6 us
    pallas_call x1, Pallas kernels, project(): pl.pallas_call(functools.partial(project_kernel, masks, shard, group), gr...  8.71 us
    unnamed x27, local copies, waits for them, and re-layouts  4.96 us
  transfers between devices with their start and end apart: 31, of which 6 were waited for; matrix products, arithmetic and copies ran while one was open for 3% of the time, Pallas kernels for 18%

profile of v2, /device:TPU:7, one launch (start us, length us, event | category | flops | bytes accessed | tf_op | source)
XLA Modules:
  0.0 178.6 jit_solution(2778454721804342210)
XLA Ops:
  1.3 1.4 collective-permute-start.23
  3.9 1.4 collective-permute-start.27
  5.3 1.5 collective-permute-start.17
  7.5 18.6 %collective-permute-done = bf16[96,1536]{1,0:T(8,128)(2,1)S(1)} collective-permute-done((bf16[96,1536]{1,0:T(8,128)(2,1)}, bf16[96,1536]{1,0:T(8,128)(2,1)S(1)}, u32[]{:S(2)}, u32[]{:S(2)}) %collective-permute-start) | collective-permute-done | bytes 294944 | tf_op jit(solution)/shard_map/ppermute | solution.py:250
  26.8 7.7 %collective-permute-done.27.refs_3_ = bf16[2,384,256]{2,1,0:T(8,128)(2,1)S(1)} collective-permute-done((bf16[2,384,256]{2,1,0:T(8,128)(2,1)S(1)}, bf16[2,384,256]{2,1,0:T(8,128)(2,1)S(1)}, u32[]{:S(2)}, u32[]{:S(2)}) %collective-permute-start.27) | collective-permute-done | bytes 393248 | tf_op jit(solution)/shard_map/ppermute | solution.py:250
  35.3 1.8 %pad_maximum_fusion.refs_0_ = bf16[192,1536]{1,0:T(8,128)(2,1)} fusion(bf16[96,1536]{1,0:T(8,128)(2,1)S(1)} %collective-permute-done, bf16[96,1536]{1,0:T(8,128)(2,1)} %bitcast.15), kind=kLoop, calls=%fused_computation | loop fusion | flops 1179648 | bytes 1179648 | tf_op jit(solution)/shard_map/concatenate | solution.py:257
  37.9 1.5 collective-permute-start.1
  42.5 13.7 %collective-permute-start.19 = (bf16[2,384,768]{2,1,0:T(8,128)(2,1)}, bf16[2,384,768]{2,1,0:T(8,128)(2,1)}, u32[]{:S(2)}, u32[]{:S(2)}) collective-permute-start(bf16[2,384,768]{2,1,0:T(8,128)(2,1)} %slice.12), channel_id=1, source_target_pairs={{0,8},{8,0},{1,9},{9,1},{2,10},{10,2},{3,11},{11,3},{4,12},{12,4},... | collective-permute-start | bytes 3538952 | tf_op jit(solution)/shard_map/ppermute | solution.py:250
  56.2 1.7 collective-permute-start.20
  58.1 4.9 %collective-permute-start.9 = (bf16[192,1536]{1,0:T(8,128)(2,1)}, bf16[192,1536]{1,0:T(8,128)(2,1)}, u32[]{:S(2)}, u32[]{:S(2)}) collective-permute-start(bf16[192,1536]{1,0:T(8,128)(2,1)} %pad_maximum_fusion.refs_0_), channel_id=1, source_target_pairs={{0,1},{1,0},{2,3},{3,2},{4,5},{5,4},{6,7},{7,6},{8,9},{9,8},{10,11... | collective-permute-start | bytes 1769480 | tf_op jit(solution)/shard_map/ppermute | solution.py:250
  65.1 1.7 copy-done.2
  66.8 11.1 %attend.4 = (bf16[1632,384]{1,0:T(8,128)(2,1)S(1)}, bf16[1632,384]{1,0:T(8,128)(2,1)S(1)}, bf16[1632,384]{1,0:T(8,128)(2,1)S(1)}) custom-call(s32[32,1]{1,0:T(8,128)S(1)} %copy.6.visible, bf16[384,1536]{1,0:T(8,128)(2,1)S(1)} %bitcast.6, bf16[384,1536]{1,0:T(8,128)(2,1)S(1)} %collective-permute-done.17.refs_1_, ...), custom_call_target="tpu_custom_call" | custom-call | flops 2717908992 | bytes 9437184 | tf_op jit(solution)/shard_map/attend/pallas_call | solution.py:109
  77.9 3.5 %attend.7 = (bf16[272,384]{1,0:T(8,128)(2,1)S(1)}, bf16[272,384]{1,0:T(8,128)(2,1)S(1)}, bf16[272,384]{1,0:T(8,128)(2,1)S(1)}) custom-call(s32[32,1]{1,0:T(8,128)S(1)} %copy.6.visible, bf16[384,1536]{1,0:T(8,128)(2,1)S(1)} %bitcast.7, bf16[384,1536]{1,0:T(8,128)(2,1)S(1)} %collective-permute-done.17.refs_1_, ...), custom_call_target="tpu_custom_call" | custom-call | flops 905969664 | bytes 2555904 | tf_op jit(solution)/shard_map/attend/pallas_call | solution.py:109
  83.1 8.1 %collective-permute-done.2 = bf16[192,1536]{1,0:T(8,128)(2,1)} collective-permute-done((bf16[192,1536]{1,0:T(8,128)(2,1)}, bf16[192,1536]{1,0:T(8,128)(2,1)}, u32[]{:S(2)}, u32[]{:S(2)}) %collective-permute-start.2) | collective-permute-done | bytes 589856 | tf_op jit(solution)/shard_map/ppermute | solution.py:250
  91.1 4.9 %collective-permute-start.29 = (bf16[272,384]{1,0:T(8,128)(2,1)S(1)}, bf16[272,384]{1,0:T(8,128)(2,1)S(1)}, u32[]{:S(2)}, u32[]{:S(2)}) collective-permute-start(bf16[272,384]{1,0:T(8,128)(2,1)S(1)} %get-tuple-element.27), channel_id=1, source_target_pairs={{0,1},{1,0},{2,3},{3,2},{4,5},{5,4},{6,7},{7,6},{8,9},{9,8},{10,11... | collective-permute-start | bytes 626696 | tf_op jit(solution)/shard_map/ppermute | solution.py:250
  98.3 6.2 %attend.6 = (bf16[544,384]{1,0:T(8,128)(2,1)S(1)}, bf16[544,384]{1,0:T(8,128)(2,1)S(1)}, bf16[544,384]{1,0:T(8,128)(2,1)S(1)}) custom-call(s32[32,1]{1,0:T(8,128)S(1)} %copy.6.visible, bf16[384,1536]{1,0:T(8,128)(2,1)S(1)} %bitcast.8, bf16[384,1536]{1,0:T(8,128)(2,1)S(1)} %collective-permute-done.17.refs_1_, ...), custom_call_target="tpu_custom_call" | custom-call | flops 1811939328 | bytes 5111808 | tf_op jit(solution)/shard_map/attend/pallas_call | solution.py:109
  104.6 12.1 %collective-permute-start.25 = (bf16[544,384]{1,0:T(8,128)(2,1)S(1)}, bf16[544,384]{1,0:T(8,128)(2,1)S(1)}, u32[]{:S(2)}, u32[]{:S(2)}) collective-permute-start(bf16[544,384]{1,0:T(8,128)(2,1)S(1)} %get-tuple-element.24), channel_id=1, source_target_pairs={{0,1},{1,0},{2,3},{3,2},{4,5},{5,4},{6,7},{7,6},{8,9},{9,8},{10,11... | collective-permute-start | bytes 1253384 | tf_op jit(solution)/shard_map/ppermute | solution.py:250
  116.7 9.8 %attend.5 = (bf16[816,384]{1,0:T(8,128)(2,1)S(1)}, bf16[816,384]{1,0:T(8,128)(2,1)S(1)}, bf16[816,384]{1,0:T(8,128)(2,1)S(1)}) custom-call(s32[32,1]{1,0:T(8,128)S(1)} %copy.6.visible, bf16[384,1536]{1,0:T(8,128)(2,1)S(1)} %bitcast.9, bf16[384,1536]{1,0:T(8,128)(2,1)S(1)} %collective-permute-done.17.refs_1_, ...), custom_call_target="tpu_custom_call" | custom-call | flops 2717908992 | bytes 7667712 | tf_op jit(solution)/shard_map/attend/pallas_call | solution.py:109
  127.5 3.1 %collective-permute-start.6 = (bf16[192,1536]{1,0:T(8,128)(2,1)S(1)}, bf16[192,1536]{1,0:T(8,128)(2,1)S(1)}, u32[]{:S(2)}, u32[]{:S(2)}) collective-permute-start(bf16[192,1536]{1,0:T(8,128)(2,1)S(1)} %broadcast_select_fusion.refs_1_), channel_id=1, source_target_pairs={{0,4},{1,5},{2,6},{3,7},{4,0},{5,1},{6,2},{7,3},{8,12},{9,13},{10,... | collective-permute-start | bytes 1769480 | tf_op jit(solution)/shard_map/ppermute | solution.py:250
  131.5 21.1 %collective-permute-start.10 = (bf16[192,1536]{1,0:T(8,128)(2,1)S(1)}, bf16[192,1536]{1,0:T(8,128)(2,1)S(1)}, u32[]{:S(2)}, u32[]{:S(2)}) collective-permute-start(bf16[192,1536]{1,0:T(8,128)(2,1)S(1)} %broadcast_select_fusion.refs_1_), channel_id=1, source_target_pairs={{0,1},{1,0},{2,3},{3,2},{4,5},{5,4},{6,7},{7,6},{8,9},{9,8},{10,11... | collective-permute-start | bytes 1769480 | tf_op jit(solution)/shard_map/ppermute | solution.py:250
  153.1 1.4 collective-permute-done.6.refs_5_
  154.5 1.4 collective-permute-start.14
  155.9 11.3 %collective-permute-done.8.refs_7_ = bf16[192,1536]{1,0:T(8,128)(2,1)S(1)} collective-permute-done((bf16[192,1536]{1,0:T(8,128)(2,1)S(1)}, bf16[192,1536]{1,0:T(8,128)(2,1)S(1)}, u32[]{:S(2)}, u32[]{:S(2)}) %collective-permute-start.8) | collective-permute-done | bytes 589856 | tf_op jit(solution)/shard_map/ppermute | solution.py:250
  169.7 8.7 %project.1 = bf16[384,3072]{1,0:T(8,128)(2,1)} custom-call(bf16[192,1536]{1,0:T(8,128)(2,1)} %pad_maximum_fusion.refs_0_, bf16[192,1536]{1,0:T(8,128)(2,1)S(1)} %broadcast_select_fusion.refs_1_, bf16[192,1536]{1,0:T(8,128)(2,1)S(1)} %copy-done.12, bf16[192,1536]{1,0:T(8,128)(2,1)S(1)} %collective-permute-done.4.refs_3_, ...), custom_call_target="tpu_custom_call" | custom-call | flops 3623878656 | bytes 9437184 | tf_op jit(solution)/shard_map/project/pallas_call | solution.py:228
  (76 shorter events, 19.3 us)
Async XLA Ops:
  1.3 38.0 %collective-permute-start.23 = (bf16[2,384,512]{2,1,0:T(8,128)(2,1)S(1)}, bf16[2,384,512]{2,1,0:T(8,128)(2,1)S(1)}, u32[]{:S(2)}, u32[]{:S(2)}) collective-permute-start(bf16[2,384,512]{2,1,0:T(8,128)(2,1)S(1)} %slice.13), channel_id=1, source_target_pairs={{0,8},{8,0},{1,9},{9,1},{2,10},{10,2},{3,11},{11,3},{4,12},{12,4},... | collective-permute-start | bytes 2359304 | tf_op jit(solution)/shard_map/ppermute | solution.py:250
  2.7 23.4 %collective-permute-start = (bf16[96,1536]{1,0:T(8,128)(2,1)}, bf16[96,1536]{1,0:T(8,128)(2,1)S(1)}, u32[]{:S(2)}, u32[]{:S(2)}) collective-permute-start(bf16[96,1536]{1,0:T(8,128)(2,1)} %bitcast.14), channel_id=1, source_target_pairs={{0,8},{8,0},{1,9},{9,1},{2,10},{10,2},{3,11},{11,3},{4,12},{12,4},... | collective-permute-start | bytes 884744 | tf_op jit(solution)/shard_map/ppermute | solution.py:250
  3.9 30.7 %collective-permute-start.27 = (bf16[2,384,256]{2,1,0:T(8,128)(2,1)S(1)}, bf16[2,384,256]{2,1,0:T(8,128)(2,1)S(1)}, u32[]{:S(2)}, u32[]{:S(2)}) collective-permute-start(bf16[2,384,256]{2,1,0:T(8,128)(2,1)S(1)} %slice.14), channel_id=1, source_target_pairs={{0,8},{8,0},{1,9},{9,1},{2,10},{10,2},{3,11},{11,3},{4,12},{12,4},... | collective-permute-start | bytes 1179656 | tf_op jit(solution)/shard_map/ppermute | solution.py:250
  5.3 52.9 %collective-permute-start.17 = (bf16[384,1536]{1,0:T(8,128)(2,1)S(1)}, bf16[384,1536]{1,0:T(8,128)(2,1)S(1)}, u32[]{:S(2)}, u32[]{:S(2)}) collective-permute-start(bf16[384,1536]{1,0:T(8,128)(2,1)S(1)} %bitcast.4), channel_id=1, source_target_pairs={{0,1},{1,0},{2,3},{3,2},{4,5},{5,4},{6,7},{7,6},{8,9},{9,8},{10,11... | collective-permute-start | bytes 3538952 | tf_op jit(solution)/shard_map/ppermute | solution.py:250
  6.8 56.3 %collective-permute-start.18 = (bf16[384,1536]{1,0:T(8,128)(2,1)S(1)}, bf16[384,1536]{1,0:T(8,128)(2,1)S(1)}, u32[]{:S(2)}, u32[]{:S(2)}) collective-permute-start(bf16[384,1536]{1,0:T(8,128)(2,1)S(1)} %bitcast.5), channel_id=1, source_target_pairs={{1,2},{2,1},{3,4},{4,3},{5,6},{6,5},{9,10},{10,9},{11,12},{12,11},... | collective-permute-start | bytes 3538952 | tf_op jit(solution)/shard_map/ppermute | solution.py:250
  37.9 18.3 %collective-permute-start.1 = (bf16[192,1536]{1,0:T(8,128)(2,1)}, bf16[192,1536]{1,0:T(8,128)(2,1)}, u32[]{:S(2)}, u32[]{:S(2)}) collective-permute-start(bf16[192,1536]{1,0:T(8,128)(2,1)} %pad_maximum_fusion.refs_0_), channel_id=1, source_target_pairs={{8,16},{16,8},{9,17},{17,9},{10,18},{18,10},{11,19},{19,11},{12,20... | collective-permute-start | bytes 1769480 | tf_op jit(solution)/shard_map/ppermute | solution.py:250
  40.3 17.6 %collective-permute-start.3 = (bf16[192,1536]{1,0:T(8,128)(2,1)}, bf16[192,1536]{1,0:T(8,128)(2,1)S(1)}, u32[]{:S(2)}, u32[]{:S(2)}) collective-permute-start(bf16[192,1536]{1,0:T(8,128)(2,1)} %pad_maximum_fusion.refs_0_), channel_id=1, source_target_pairs={{0,2},{1,3},{2,0},{3,1},{4,6},{5,7},{6,4},{7,5},{8,10},{9,11},{10,... | collective-permute-start | bytes 1769480 | tf_op jit(solution)/shard_map/ppermute | solution.py:250
  42.5 54.7 %collective-permute-start.19 = (bf16[2,384,768]{2,1,0:T(8,128)(2,1)}, bf16[2,384,768]{2,1,0:T(8,128)(2,1)}, u32[]{:S(2)}, u32[]{:S(2)}) collective-permute-start(bf16[2,384,768]{2,1,0:T(8,128)(2,1)} %slice.12), channel_id=1, source_target_pairs={{0,8},{8,0},{1,9},{9,1},{2,10},{10,2},{3,11},{11,3},{4,12},{12,4},... | collective-permute-start | bytes 3538952 | tf_op jit(solution)/shard_map/ppermute | solution.py:250
  56.2 41.1 %collective-permute-start.20 = (bf16[2,384,768]{2,1,0:T(8,128)(2,1)}, bf16[2,384,768]{2,1,0:T(8,128)(2,1)}, u32[]{:S(2)}, u32[]{:S(2)}) collective-permute-start(bf16[2,384,768]{2,1,0:T(8,128)(2,1)} %slice.12), channel_id=1, source_target_pairs={{8,16},{16,8},{9,17},{17,9},{10,18},{18,10},{11,19},{19,11},{12,20... | collective-permute-start | bytes 3538952 | tf_op jit(solution)/shard_map/ppermute | solution.py:250
  57.9 23.5 %collective-permute-start.5 = (bf16[192,1536]{1,0:T(8,128)(2,1)}, bf16[192,1536]{1,0:T(8,128)(2,1)}, u32[]{:S(2)}, u32[]{:S(2)}) collective-permute-start(bf16[192,1536]{1,0:T(8,128)(2,1)} %pad_maximum_fusion.refs_0_), channel_id=1, source_target_pairs={{0,4},{1,5},{2,6},{3,7},{4,0},{5,1},{6,2},{7,3},{8,12},{9,13},{10,... | collective-permute-start | bytes 1769480 | tf_op jit(solution)/shard_map/ppermute | solution.py:250
  58.1 24.6 %collective-permute-start.9 = (bf16[192,1536]{1,0:T(8,128)(2,1)}, bf16[192,1536]{1,0:T(8,128)(2,1)}, u32[]{:S(2)}, u32[]{:S(2)}) collective-permute-start(bf16[192,1536]{1,0:T(8,128)(2,1)} %pad_maximum_fusion.refs_0_), channel_id=1, source_target_pairs={{0,1},{1,0},{2,3},{3,2},{4,5},{5,4},{6,7},{7,6},{8,9},{9,8},{10,11... | collective-permute-start | bytes 1769480 | tf_op jit(solution)/shard_map/ppermute | solution.py:250
  63.1 28.1 %collective-permute-start.2 = (bf16[192,1536]{1,0:T(8,128)(2,1)}, bf16[192,1536]{1,0:T(8,128)(2,1)}, u32[]{:S(2)}, u32[]{:S(2)}) collective-permute-start(bf16[192,1536]{1,0:T(8,128)(2,1)} %collective-permute-done.1), channel_id=1, source_target_pairs={{8,0},{9,1},{10,2},{11,3},{12,4},{13,5},{14,6},{15,7},{16,24},{17,... | collective-permute-start | bytes 1769480 | tf_op jit(solution)/shard_map/ppermute | solution.py:250
  81.5 45.1 %collective-permute-start.7 = (bf16[192,1536]{1,0:T(8,128)(2,1)S(1)}, bf16[192,1536]{1,0:T(8,128)(2,1)S(1)}, u32[]{:S(2)}, u32[]{:S(2)}) collective-permute-start(bf16[192,1536]{1,0:T(8,128)(2,1)S(1)} %copy-done.12), channel_id=1, source_target_pairs={{0,4},{1,5},{2,6},{3,7},{4,0},{5,1},{6,2},{7,3},{8,12},{9,13},{10,... | collective-permute-start | bytes 1769480 | tf_op jit(solution)/shard_map/ppermute | solution.py:250
  82.8 43.8 %collective-permute-start.11 = (bf16[192,1536]{1,0:T(8,128)(2,1)S(1)}, bf16[192,1536]{1,0:T(8,128)(2,1)S(1)}, u32[]{:S(2)}, u32[]{:S(2)}) collective-permute-start(bf16[192,1536]{1,0:T(8,128)(2,1)S(1)} %copy-done.12), channel_id=1, source_target_pairs={{0,1},{1,0},{2,3},{3,2},{4,5},{5,4},{6,7},{7,6},{8,9},{9,8},{10,11... | collective-permute-start | bytes 1769480 | tf_op jit(solution)/shard_map/ppermute | solution.py:250
  97.2 30.3 %collective-permute-start.13 = (bf16[192,1536]{1,0:T(8,128)(2,1)}, bf16[192,1536]{1,0:T(8,128)(2,1)S(1)}, u32[]{:S(2)}, u32[]{:S(2)}) collective-permute-start(bf16[192,1536]{1,0:T(8,128)(2,1)} %collective-permute-done.5.refs_4_), channel_id=1, source_target_pairs={{0,1},{1,0},{2,3},{3,2},{4,5},{5,4},{6,7},{7,6},{8,9},{9,8},{10,11... | collective-permute-start | bytes 1769480 | tf_op jit(solution)/shard_map/ppermute | solution.py:250
  97.3 33.4 %collective-permute-start.4 = (bf16[192,1536]{1,0:T(8,128)(2,1)S(1)}, bf16[192,1536]{1,0:T(8,128)(2,1)S(1)}, u32[]{:S(2)}, u32[]{:S(2)}) collective-permute-start(bf16[192,1536]{1,0:T(8,128)(2,1)S(1)} %broadcast_select_fusion.refs_1_), channel_id=1, source_target_pairs={{0,2},{1,3},{2,0},{3,1},{4,6},{5,7},{6,4},{7,5},{8,10},{9,11},{10,... | collective-permute-start | bytes 1769480 | tf_op jit(solution)/shard_map/ppermute | solution.py:250
  104.6 26.2 %collective-permute-start.25 = (bf16[544,384]{1,0:T(8,128)(2,1)S(1)}, bf16[544,384]{1,0:T(8,128)(2,1)S(1)}, u32[]{:S(2)}, u32[]{:S(2)}) collective-permute-start(bf16[544,384]{1,0:T(8,128)(2,1)S(1)} %get-tuple-element.24), channel_id=1, source_target_pairs={{0,1},{1,0},{2,3},{3,2},{4,5},{5,4},{6,7},{7,6},{8,9},{9,8},{10,11... | collective-permute-start | bytes 1253384 | tf_op jit(solution)/shard_map/ppermute | solution.py:250
  126.5 26.0 %collective-permute-start.21 = (bf16[816,384]{1,0:T(8,128)(2,1)S(1)}, bf16[816,384]{1,0:T(8,128)(2,1)S(1)}, u32[]{:S(2)}, u32[]{:S(2)}) collective-permute-start(bf16[816,384]{1,0:T(8,128)(2,1)S(1)} %get-tuple-element.21), channel_id=1, source_target_pairs={{0,1},{1,0},{2,3},{3,2},{4,5},{5,4},{6,7},{7,6},{8,9},{9,8},{10,11... | collective-permute-start | bytes 1880072 | tf_op jit(solution)/shard_map/ppermute | solution.py:250
  126.6 26.0 %collective-permute-start.22 = (bf16[816,384]{1,0:T(8,128)(2,1)S(1)}, bf16[816,384]{1,0:T(8,128)(2,1)S(1)}, u32[]{:S(2)}, u32[]{:S(2)}) collective-permute-start(bf16[816,384]{1,0:T(8,128)(2,1)S(1)} %get-tuple-element.22), channel_id=1, source_target_pairs={{1,2},{2,1},{3,4},{4,3},{5,6},{6,5},{9,10},{10,9},{11,12},{12,11},... | collective-permute-start | bytes 1880072 | tf_op jit(solution)/shard_map/ppermute | solution.py:250
  127.5 27.0 %collective-permute-start.6 = (bf16[192,1536]{1,0:T(8,128)(2,1)S(1)}, bf16[192,1536]{1,0:T(8,128)(2,1)S(1)}, u32[]{:S(2)}, u32[]{:S(2)}) collective-permute-start(bf16[192,1536]{1,0:T(8,128)(2,1)S(1)} %broadcast_select_fusion.refs_1_), channel_id=1, source_target_pairs={{0,4},{1,5},{2,6},{3,7},{4,0},{5,1},{6,2},{7,3},{8,12},{9,13},{10,... | collective-permute-start | bytes 1769480 | tf_op jit(solution)/shard_map/ppermute | solution.py:250
  130.7 36.5 %collective-permute-start.8 = (bf16[192,1536]{1,0:T(8,128)(2,1)S(1)}, bf16[192,1536]{1,0:T(8,128)(2,1)S(1)}, u32[]{:S(2)}, u32[]{:S(2)}) collective-permute-start(bf16[192,1536]{1,0:T(8,128)(2,1)S(1)} %collective-permute-done.4.refs_3_), channel_id=1, source_target_pairs={{0,4},{1,5},{2,6},{3,7},{4,0},{5,1},{6,2},{7,3},{8,12},{9,13},{10,... | collective-permute-start | bytes 1769480 | tf_op jit(solution)/shard_map/ppermute | solution.py:250
  131.5 37.5 %collective-permute-start.10 = (bf16[192,1536]{1,0:T(8,128)(2,1)S(1)}, bf16[192,1536]{1,0:T(8,128)(2,1)S(1)}, u32[]{:S(2)}, u32[]{:S(2)}) collective-permute-start(bf16[192,1536]{1,0:T(8,128)(2,1)S(1)} %broadcast_select_fusion.refs_1_), channel_id=1, source_target_pairs={{0,1},{1,0},{2,3},{3,2},{4,5},{5,4},{6,7},{7,6},{8,9},{9,8},{10,11... | collective-permute-start | bytes 1769480 | tf_op jit(solution)/shard_map/ppermute | solution.py:250
  152.6 16.4 %collective-permute-start.15 = (bf16[192,1536]{1,0:T(8,128)(2,1)S(1)}, bf16[192,1536]{1,0:T(8,128)(2,1)S(1)}, u32[]{:S(2)}, u32[]{:S(2)}) collective-permute-start(bf16[192,1536]{1,0:T(8,128)(2,1)S(1)} %collective-permute-done.7.refs_6_), channel_id=1, source_target_pairs={{0,1},{1,0},{2,3},{3,2},{4,5},{5,4},{6,7},{7,6},{8,9},{9,8},{10,11... | collective-permute-start | bytes 1769480 | tf_op jit(solution)/shard_map/ppermute | solution.py:250
  152.6 16.4 %collective-permute-start.12 = (bf16[192,1536]{1,0:T(8,128)(2,1)S(1)}, bf16[192,1536]{1,0:T(8,128)(2,1)S(1)}, u32[]{:S(2)}, u32[]{:S(2)}) collective-permute-start(bf16[192,1536]{1,0:T(8,128)(2,1)S(1)} %collective-permute-done.4.refs_3_), channel_id=1, source_target_pairs={{0,1},{1,0},{2,3},{3,2},{4,5},{5,4},{6,7},{7,6},{8,9},{9,8},{10,11... | collective-permute-start | bytes 1769480 | tf_op jit(solution)/shard_map/ppermute | solution.py:250
  (20 other events, 168.7 us)
